TPU v7x, 256 devices: a whole 4x4x8 slice. The times are simulated.
256 devices in a mesh: patch: 16 (over z, x_hi), sub: 16 (over x_lo, y, core).
Axes of the slice: x: 4 (x_hi: 2, x_lo: 2; x = x_hi * 2 + x_lo), y: 4, z: 8, core: 2. Of those that a mesh axis runs over, the one named last changes fastest.
Arguments:
- displacement: float32 [3, 128, 32768], P(None, 'patch', 'sub'), may hold values from -3 to 3
- load: float32 [3, 128, 32768], P(None, 'patch', 'sub'), may hold values from -6 to 6
- foundation: float32 [3, 128, 32768], P(None, 'patch', 'sub'), may hold values from 0.2 to 2
- layup: int32 [128, 32768], P('patch', 'sub'), may hold values from 0 to 7
- layup_stiffness: float32 [8, 6, 6], replicated, as said below
- w_first: bfloat16 [128, 6], replicated, may hold values from -2.5 to 2.5
- w_mid: bfloat16 [3, 128, 128], replicated, may hold values from -0.5 to 0.5
- w_last: bfloat16 [6, 128], replicated, may hold values from -0.5 to 0.5
Outputs:
- residual: float32 [3, 128, 32768], P(None, 'patch', 'sub')
- adjoint: float32 [3, 128, 32768], P(None, 'patch', 'sub')
- grad_first: float32 [128, 6], replicated
- grad_mid: float32 [3, 128, 128], replicated
- grad_last: float32 [6, 128], replicated
Inputs may be any that keep to these rules, and one draw needn't show every extreme that they name: `layup_stiffness`: each of the 8 matrices is symmetric positive definite.
All inputs are finite; a program needn't handle non-finite values.
Results may differ from a plain program's by a relative error of at most 0.0006.
The roundings to bfloat16 on the way count: a program that leaves them out, or rounds other values in their place, can miss the bound.
Values sent between devices are 32-bit elements; how exact they have to be, the bound alone decides.
A program may use at most 128 MiB of HBM per device.

v0:
```python
import functools

import jax
import jax.numpy as jnp
from jax import lax
from jax.sharding import Mesh
from jax.sharding import PartitionSpec as P

ITERS = 4
PATCH_SUB = ("patch_0", "patch_1", "sub_0", "sub_1", "sub_2")
PATCH = ("patch_0", "patch_1")
SUB = ("sub_0", "sub_1", "sub_2")


BASIS_VALUE = (0.125, 0.75, 0.125)
BASIS_SLOPE = (-0.5, 0.0, 0.5)
BASIS_CURVE = (1.0, -2.0, 1.0)
HOOP_CURVATURE = 0.25


def by_axis(value, axes):
    return functools.reduce(lax.psum, axes, value)


def padded_2(cells, sides, width):
    for axis, dim in sides:
        count = lax.axis_size(axis)
        head = lax.slice_in_dim(cells, 0, width, axis=dim)
        tail = lax.slice_in_dim(cells, cells.shape[dim] - width, cells.shape[dim], axis=dim)
        cells = jnp.concatenate(
            [
                lax.ppermute(tail, axis, [(i, (i + 1) % count) for i in range(count)]),
                cells,
                lax.ppermute(head, axis, [((i + 1) % count, i) for i in range(count)]),
            ],
            axis=dim,
        )
    return cells


def split_up(value, dim, size):
    lengths = value.shape
    pieces = value.reshape(*lengths[:dim], size, lengths[dim] // size, *lengths[dim + 1 :])
    return jnp.moveaxis(pieces, dim, 0)


def sent_and_summed(value, axis, dim):
    size = lax.axis_size(axis)
    pieces = lax.all_to_all(split_up(value, dim, size), axis, 0, 0, tiled=True)
    return jnp.sum(pieces, axis=0)


def sent_to_all(value, axis):
    size = lax.axis_size(axis)
    return lax.all_to_all(
        jnp.broadcast_to(value[None], (size, *value.shape)), axis, 0, 0, tiled=True
    )


def of_everyone(value, axis):
    return sent_to_all(value, axis).sum(axis=0)


def packed_total(arrays, axis):
    vector, at, done = (jnp.concatenate([a.reshape(-1) for a in arrays]), 0, [])
    subtotal = of_everyone(vector, axis)
    for a in arrays:
        done.append(subtotal[at : at + a.size].reshape(a.shape))
        at += a.size
    return tuple(done)


def turned_gather(arrays, axis, dims):
    turned = [jnp.moveaxis(a, dim, 0) for a, dim in zip(arrays, dims)]
    both = jnp.concatenate([t.reshape(len(t), -1) for t in turned], axis=1)
    filled, at, done = (lax.all_gather(both, axis, axis=0, tiled=True), 0, [])
    for t, dim in zip(turned, dims):
        section = filled[:, at : at + t[0].size].reshape(-1, *t.shape[1:])
        done.append(jnp.moveaxis(section, 0, dim))
        at += t[0].size
    return tuple(done)


def correlate(padded, along_x, along_y):
    row_count = padded.shape[-2] - 2
    col_count = padded.shape[-1] - 2
    partial_x = None
    for offset in range(3):
        if along_x[offset] != 0.0:
            weighted = along_x[offset] * padded[..., offset : offset + row_count, :]
            partial_x = weighted if partial_x is None else partial_x + weighted
    running = None
    for offset in range(3):
        if along_y[offset] != 0.0:
            weighted = along_y[offset] * partial_x[..., offset : offset + col_count]
            running = weighted if running is None else running + weighted
    return running


def mirrored(padded, along_x, along_y):
    return correlate(padded, along_x[::-1], along_y[::-1])


def strains(padded):
    along_u, along_v, along_w = (padded[0], padded[1], padded[2])
    return jnp.stack(
        [
            correlate(along_u, BASIS_SLOPE, BASIS_VALUE),
            correlate(along_v, BASIS_VALUE, BASIS_SLOPE)
            + HOOP_CURVATURE * correlate(along_w, BASIS_VALUE, BASIS_VALUE),
            correlate(along_u, BASIS_VALUE, BASIS_SLOPE)
            + correlate(along_v, BASIS_SLOPE, BASIS_VALUE),
            -correlate(along_w, BASIS_CURVE, BASIS_VALUE),
            -correlate(along_w, BASIS_VALUE, BASIS_CURVE),
            -2.0 * correlate(along_w, BASIS_SLOPE, BASIS_SLOPE),
        ]
    )


def forces(spread):
    force_u = mirrored(spread[0], BASIS_SLOPE, BASIS_VALUE) + mirrored(
        spread[2], BASIS_VALUE, BASIS_SLOPE
    )
    force_v = mirrored(spread[1], BASIS_VALUE, BASIS_SLOPE) + mirrored(
        spread[2], BASIS_SLOPE, BASIS_VALUE
    )
    force_w = (
        HOOP_CURVATURE * mirrored(spread[1], BASIS_VALUE, BASIS_VALUE)
        - mirrored(spread[3], BASIS_CURVE, BASIS_VALUE)
        - mirrored(spread[4], BASIS_VALUE, BASIS_CURVE)
        - 2.0 * mirrored(spread[5], BASIS_SLOPE, BASIS_SLOPE)
    )
    return jnp.stack([force_u, force_v, force_w])


def apply_layup(stiffness_map, strain):
    running = stiffness_map[:, 0] * strain[0]
    for column in range(1, 6):
        running = running + stiffness_map[:, column] * strain[column]
    return running


def outer_product(left, right):
    return lax.dot_general(
        left, right, (((1,), (1,)), ((), ())), preferred_element_type=jnp.float32
    )


def forward_mlp(inputs, w_first, w_mid, w_last):
    hidden_layer = jnp.tanh(jnp.dot(w_first, inputs, preferred_element_type=jnp.float32)).astype(
        jnp.bfloat16
    )
    activations = [hidden_layer]
    for layer_index in range(w_mid.shape[0]):
        hidden_layer = jnp.tanh(
            jnp.dot(w_mid[layer_index], hidden_layer, preferred_element_type=jnp.float32)
        ).astype(jnp.bfloat16)
        activations.append(hidden_layer)
    return (jnp.dot(w_last, hidden_layer, preferred_element_type=jnp.float32), activations)


def backward_mlp(inputs, activations, upstream, w_mid, w_last):
    grad_last = outer_product(upstream, activations[-1])
    signal = jnp.dot(w_last.T, upstream, preferred_element_type=jnp.float32)
    derivative = (signal * (1.0 - jnp.square(activations[-1].astype(jnp.float32)))).astype(
        jnp.bfloat16
    )
    mid_grads = []
    for layer_index in range(w_mid.shape[0] - 1, -1, -1):
        mid_grads.append(outer_product(derivative, activations[layer_index]))
        signal = jnp.dot(w_mid[layer_index].T, derivative, preferred_element_type=jnp.float32)
        derivative = (
            signal * (1.0 - jnp.square(activations[layer_index].astype(jnp.float32)))
        ).astype(jnp.bfloat16)
    grad_first = outer_product(derivative, inputs)
    return (grad_first, jnp.stack(mid_grads[::-1]), grad_last)


def two_products(remainder, mapped):
    return (
        by_axis(jnp.sum(remainder * remainder), PATCH_SUB),
        by_axis(jnp.sum(remainder * mapped), PATCH_SUB),
    )


def per_device(displacement, load, foundation, layup, layup_stiffness, w_first, w_mid, w_last):
    layup_count = layup_stiffness.shape[0]

    def coefficients(layup_ids):
        onehot = (
            layup_ids[None] == jnp.arange(layup_count, dtype=jnp.int32)[:, None, None]
        ).astype(jnp.float32)
        return jnp.einsum("lab,lxy->abxy", layup_stiffness, onehot, precision=lax.Precision.HIGHEST)

    stiffness_map = coefficients(layup)
    wide_ids = padded_2(layup, ((PATCH, 0), (SUB, 1)), 1)
    stiffness_wide = coefficients(wide_ids)

    def operate(search):
        padded = padded_2(search, ((PATCH, 1), (SUB, 2)), 2)
        return forces(apply_layup(stiffness_wide, strains(padded))) + foundation * search

    padded = padded_2(displacement, ((PATCH, 1), (SUB, 2)), 1)
    strain = strains(padded)
    inputs = strain.reshape(6, -1).astype(jnp.bfloat16)
    learned, activations = forward_mlp(inputs, w_first, w_mid, w_last)
    stress = apply_layup(stiffness_map, strain) + learned.reshape(strain.shape)
    spread = padded_2(stress, ((PATCH, 1), (SUB, 2)), 1)
    residual = forces(spread) + foundation * displacement - load
    adjoint = jnp.zeros_like(residual)
    remainder = residual
    mapped = operate(remainder)
    norm_now, curved = two_products(remainder, mapped)
    step_size = norm_now / curved
    direction, mapped_dir = (remainder, mapped)
    for step_index in range(ITERS):
        adjoint = adjoint + step_size * direction
        remainder = remainder - step_size * mapped_dir
        if step_index + 1 < ITERS:
            mapped = operate(remainder)
            norm_next, curved = two_products(remainder, mapped)
            beta_ratio = norm_next / norm_now
            step_size = norm_next / (curved - beta_ratio * norm_next / step_size)
            direction = remainder + beta_ratio * direction
            mapped_dir = mapped + beta_ratio * mapped_dir
            norm_now = norm_next
    cycle = padded_2(adjoint, ((PATCH, 1), (SUB, 2)), 1)
    upstream = strains(cycle).reshape(6, -1).astype(jnp.bfloat16)
    grad_first, grad_mid, grad_last = backward_mlp(inputs, activations, upstream, w_mid, w_last)
    shares = (
        sent_and_summed(grad_first, SUB, 0),
        sent_and_summed(grad_mid, SUB, 1),
        sent_and_summed(grad_last, SUB, 1),
    )
    crossed = packed_total((shares[0], shares[1], shares[2]), PATCH)
    totals = turned_gather((crossed[0], crossed[1], crossed[2]), SUB, (0, 1, 1))
    return (residual, adjoint, totals[0], totals[1], totals[2])


def solution(mesh):
    split = Mesh(
        mesh.devices.reshape(8, 2, 2, 4, 2), ("patch_0", "patch_1", "sub_0", "sub_1", "sub_2")
    )
    return jax.shard_map(
        per_device,
        mesh=split,
        in_specs=(
            P(None, PATCH, SUB),
            P(None, PATCH, SUB),
            P(None, PATCH, SUB),
            P(PATCH, SUB),
            P(),
            P(),
            P(),
            P(),
        ),
        out_specs=(P(None, PATCH, SUB), P(None, PATCH, SUB), P(), P(), P()),
        check_vma=False,
    )
```

profile of v0, /device:TPU:1, one launch (start us, length us, event | category | flops | bytes accessed | tf_op | source)
XLA Modules:
  0.0 428.8 jit_solution(17455892950688272577)
XLA Ops:
  5.4 5.4 %collective-permute-start.1 = (f32[3,1,2048]{2,1,0:T(1,128)S(1)}, f32[3,1,2048]{2,1,0:T(1,128)S(1)}, u32[]{:S(2)}, u32[]{:S(2)}) collective-permute-start(f32[3,1,2048]{2,1,0:T(1,128)S(1)} %get-tuple-element.222), channel_id=1, source_target_pairs={{16,0},{32,16},{48,32},{64,48},{80,64},{96,80},{112,96},{128,112},... | collective-permute-start | bytes 73736 | tf_op jit(solution)/shard_map/ppermute | solution.py:34
  34.2 5.1 %collective-permute-start.5 = (f32[6,1,2048]{2,1,0:T(1,128)S(1)}, f32[6,1,2048]{2,1,0:T(1,128)S(1)}, u32[]{:S(2)}, u32[]{:S(2)}) collective-permute-start(f32[6,1,2048]{2,1,0:T(1,128)S(1)} %get-tuple-element.206), channel_id=1, source_target_pairs={{16,0},{32,16},{48,32},{64,48},{80,64},{96,80},{112,96},{128,112},... | collective-permute-start | bytes 147464 | tf_op jit(solution)/shard_map/ppermute | solution.py:34
  39.4 5.3 %collective-permute-start.9 = (s32[1,2048]{1,0:T(1,128)S(1)}, s32[1,2048]{1,0:T(1,128)S(1)}, u32[]{:S(2)}, u32[]{:S(2)}) collective-permute-start(s32[1,2048]{1,0:T(1,128)S(1)} %get-tuple-element.248), channel_id=1, source_target_pairs={{16,0},{32,16},{48,32},{64,48},{80,64},{96,80},{112,96},{128,112},... | collective-permute-start | bytes 24584 | tf_op jit(solution)/shard_map/ppermute | solution.py:34
  45.0 5.2 %collective-permute-start.7 = (f32[6,10,1]{2,1,0:T(8,128)S(1)}, f32[6,10,1]{2,1,0:T(8,128)S(1)}, u32[]{:S(2)}, u32[]{:S(2)}) collective-permute-start(f32[6,10,1]{2,1,0:T(8,128)S(1)} %get-tuple-element.151), channel_id=1, source_target_pairs={{1,0},{2,1},{3,2},{4,3},{5,4},{6,5},{7,6},{8,7},{9,8},{10,9},{11,1... | collective-permute-start | bytes 728 | tf_op jit(solution)/shard_map/ppermute | solution.py:34
  52.6 5.1 %collective-permute-start.13 = (f32[3,2,2048]{2,1,0:T(2,128)S(1)}, f32[3,2,2048]{2,1,0:T(2,128)S(1)}, u32[]{:S(2)}, u32[]{:S(2)}) collective-permute-start(f32[3,2,2048]{2,1,0:T(2,128)S(1)} %get-tuple-element.220), channel_id=1, source_target_pairs={{16,0},{32,16},{48,32},{64,48},{80,64},{96,80},{112,96},{128,112},... | collective-permute-start | bytes 147464 | tf_op jit(solution)/shard_map/ppermute | solution.py:34
  57.7 5.5 %collective-permute-start.11 = (s32[10,1]{1,0:T(8,128)S(1)}, s32[10,1]{1,0:T(8,128)S(1)}, u32[]{:S(2)}, u32[]{:S(2)}) collective-permute-start(s32[10,1]{1,0:T(8,128)S(1)} %get-tuple-element.231), channel_id=1, source_target_pairs={{1,0},{2,1},{3,2},{4,3},{5,4},{6,5},{7,6},{8,7},{9,8},{10,9},{11,1... | collective-permute-start | bytes 128 | tf_op jit(solution)/shard_map/ppermute | solution.py:34
  78.5 11.8 %all-reduce.3 = (f32[]{:T(128)}, f32[]{:T(128)}) all-reduce(f32[]{:T(128)} %get-tuple-element.57, f32[]{:T(128)} %get-tuple-element.56), channel_id=1, replica_groups=mesh['patch_0'=8,'patch_1'=2,'sub_0'=2,'sub_1'=4,'sub_2'=2] {'patch_0'}, use_global_device_ids=true, to_apply=%region_1.0 | all-reduce | flops 2 | bytes 16 | tf_op jit(solution)/shard_map/psum | solution.py:22
  90.4 5.9 %all-reduce.19 = (f32[]{:T(128)}, f32[]{:T(128)}) all-reduce(f32[]{:T(128)} %get-tuple-element.64, f32[]{:T(128)} %get-tuple-element.65), channel_id=1, replica_groups=mesh['patch_0'=8,'patch_1'=2,'sub_0'=2,'sub_1'=4,'sub_2'=2] {'patch_1'}, use_global_device_ids=true, to_apply=%region_2.0 | all-reduce | flops 2 | bytes 16 | tf_op jit(solution)/shard_map/psum | solution.py:22
  96.3 4.4 %all-reduce.15 = (f32[]{:T(128)}, f32[]{:T(128)}) all-reduce(f32[]{:T(128)} %get-tuple-element.96, f32[]{:T(128)} %get-tuple-element.97), channel_id=1, replica_groups=mesh['patch_0'=8,'patch_1'=2,'sub_0'=2,'sub_1'=4,'sub_2'=2] {'sub_0'}, use_global_device_ids=true, to_apply=%region_3.0 | all-reduce | flops 2 | bytes 16 | tf_op jit(solution)/shard_map/psum | solution.py:22
  100.7 10.1 %all-reduce.7 = (f32[]{:T(128)}, f32[]{:T(128)}) all-reduce(f32[]{:T(128)} %get-tuple-element.88, f32[]{:T(128)} %get-tuple-element.89), channel_id=1, replica_groups=mesh['patch_0'=8,'patch_1'=2,'sub_0'=2,'sub_1'=4,'sub_2'=2] {'sub_1'}, use_global_device_ids=true, to_apply=%region_4.0 | all-reduce | flops 2 | bytes 16 | tf_op jit(solution)/shard_map/psum | solution.py:22
  110.8 7.2 %all-reduce.11 = (f32[]{:T(128)}, f32[]{:T(128)}) all-reduce(f32[]{:T(128)} %get-tuple-element.72, f32[]{:T(128)} %get-tuple-element.73), channel_id=1, replica_groups=mesh['patch_0'=8,'patch_1'=2,'sub_0'=2,'sub_1'=4,'sub_2'=2] {'sub_2'}, use_global_device_ids=true, to_apply=%region_5.0 | all-reduce | flops 2 | bytes 16 | tf_op jit(solution)/shard_map/psum | solution.py:22
  136.8 12.2 %all-reduce.2 = (f32[]{:T(128)}, f32[]{:T(128)}) all-reduce(f32[]{:T(128)} %get-tuple-element.55, f32[]{:T(128)} %get-tuple-element.54), channel_id=1, replica_groups=mesh['patch_0'=8,'patch_1'=2,'sub_0'=2,'sub_1'=4,'sub_2'=2] {'patch_0'}, use_global_device_ids=true, to_apply=%region_13.0 | all-reduce | flops 2 | bytes 16 | tf_op jit(solution)/shard_map/psum | solution.py:22
  149.0 6.7 %all-reduce.18 = (f32[]{:T(128)}, f32[]{:T(128)}) all-reduce(f32[]{:T(128)} %get-tuple-element.62, f32[]{:T(128)} %get-tuple-element.63), channel_id=1, replica_groups=mesh['patch_0'=8,'patch_1'=2,'sub_0'=2,'sub_1'=4,'sub_2'=2] {'patch_1'}, use_global_device_ids=true, to_apply=%region_14.0 | all-reduce | flops 2 | bytes 16 | tf_op jit(solution)/shard_map/psum | solution.py:22
  160.0 9.3 %all-reduce.6 = (f32[]{:T(128)}, f32[]{:T(128)}) all-reduce(f32[]{:T(128)} %get-tuple-element.86, f32[]{:T(128)} %get-tuple-element.87), channel_id=1, replica_groups=mesh['patch_0'=8,'patch_1'=2,'sub_0'=2,'sub_1'=4,'sub_2'=2] {'sub_1'}, use_global_device_ids=true, to_apply=%region_16.0 | all-reduce | flops 2 | bytes 16 | tf_op jit(solution)/shard_map/psum | solution.py:22
  169.3 11.9 %all-reduce.10 = (f32[]{:T(128)}, f32[]{:T(128)}) all-reduce(f32[]{:T(128)} %get-tuple-element.70, f32[]{:T(128)} %get-tuple-element.71), channel_id=1, replica_groups=mesh['patch_0'=8,'patch_1'=2,'sub_0'=2,'sub_1'=4,'sub_2'=2] {'sub_2'}, use_global_device_ids=true, to_apply=%region_17.0 | all-reduce | flops 2 | bytes 16 | tf_op jit(solution)/shard_map/psum | solution.py:22
  204.1 11.3 %all-reduce.1 = (f32[]{:T(128)}, f32[]{:T(128)}) all-reduce(f32[]{:T(128)} %get-tuple-element.53, f32[]{:T(128)} %get-tuple-element.52), channel_id=1, replica_groups=mesh['patch_0'=8,'patch_1'=2,'sub_0'=2,'sub_1'=4,'sub_2'=2] {'patch_0'}, use_global_device_ids=true, to_apply=%region_25.0 | all-reduce | flops 2 | bytes 16 | tf_op jit(solution)/shard_map/psum | solution.py:22
  215.4 7.4 %all-reduce.17 = (f32[]{:T(128)}, f32[]{:T(128)}) all-reduce(f32[]{:T(128)} %get-tuple-element.60, f32[]{:T(128)} %get-tuple-element.61), channel_id=1, replica_groups=mesh['patch_0'=8,'patch_1'=2,'sub_0'=2,'sub_1'=4,'sub_2'=2] {'patch_1'}, use_global_device_ids=true, to_apply=%region_26.0 | all-reduce | flops 2 | bytes 16 | tf_op jit(solution)/shard_map/psum | solution.py:22
  227.2 8.5 %all-reduce.5 = (f32[]{:T(128)}, f32[]{:T(128)}) all-reduce(f32[]{:T(128)} %get-tuple-element.84, f32[]{:T(128)} %get-tuple-element.85), channel_id=1, replica_groups=mesh['patch_0'=8,'patch_1'=2,'sub_0'=2,'sub_1'=4,'sub_2'=2] {'sub_1'}, use_global_device_ids=true, to_apply=%region_28.0 | all-reduce | flops 2 | bytes 16 | tf_op jit(solution)/shard_map/psum | solution.py:22
  235.7 10.7 %all-reduce.9 = (f32[]{:T(128)}, f32[]{:T(128)}) all-reduce(f32[]{:T(128)} %get-tuple-element.68, f32[]{:T(128)} %get-tuple-element.69), channel_id=1, replica_groups=mesh['patch_0'=8,'patch_1'=2,'sub_0'=2,'sub_1'=4,'sub_2'=2] {'sub_2'}, use_global_device_ids=true, to_apply=%region_29.0 | all-reduce | flops 2 | bytes 16 | tf_op jit(solution)/shard_map/psum | solution.py:22
  268.5 11.3 %all-reduce = (f32[]{:T(128)}, f32[]{:T(128)}) all-reduce(f32[]{:T(128)} %get-tuple-element.51, f32[]{:T(128)} %get-tuple-element.50), channel_id=1, replica_groups=mesh['patch_0'=8,'patch_1'=2,'sub_0'=2,'sub_1'=4,'sub_2'=2] {'patch_0'}, use_global_device_ids=true, to_apply=%region_37.0 | all-reduce | flops 2 | bytes 16 | tf_op jit(solution)/shard_map/psum | solution.py:22
  279.8 7.1 %all-reduce.16 = (f32[]{:T(128)}, f32[]{:T(128)}) all-reduce(f32[]{:T(128)} %get-tuple-element.58, f32[]{:T(128)} %get-tuple-element.59), channel_id=1, replica_groups=mesh['patch_0'=8,'patch_1'=2,'sub_0'=2,'sub_1'=4,'sub_2'=2] {'patch_1'}, use_global_device_ids=true, to_apply=%region_38.0 | all-reduce | flops 2 | bytes 16 | tf_op jit(solution)/shard_map/psum | solution.py:22
  291.3 8.8 %all-reduce.4 = (f32[]{:T(128)}, f32[]{:T(128)}) all-reduce(f32[]{:T(128)} %get-tuple-element.82, f32[]{:T(128)} %get-tuple-element.83), channel_id=1, replica_groups=mesh['patch_0'=8,'patch_1'=2,'sub_0'=2,'sub_1'=4,'sub_2'=2] {'sub_1'}, use_global_device_ids=true, to_apply=%region_40.0 | all-reduce | flops 2 | bytes 16 | tf_op jit(solution)/shard_map/psum | solution.py:22
  300.1 11.6 %all-reduce.8 = (f32[]{:T(128)}, f32[]{:T(128)}) all-reduce(f32[]{:T(128)} %get-tuple-element.66, f32[]{:T(128)} %get-tuple-element.67), channel_id=1, replica_groups=mesh['patch_0'=8,'patch_1'=2,'sub_0'=2,'sub_1'=4,'sub_2'=2] {'sub_2'}, use_global_device_ids=true, to_apply=%region_41.0 | all-reduce | flops 2 | bytes 16 | tf_op jit(solution)/shard_map/psum | solution.py:22
  342.6 5.0 %fusion.13 = f32[16,6,8]{0,1,2:T(8,128)S(1)} fusion(bf16[16,8,16384]{2,1,0:T(8,128)(2,1)S(1)} %bitcast.440, bf16[6,16384]{1,0:T(8,128)(2,1)S(1)} %stack.171), kind=kOutput, calls=%fused_computation.26 | convolution fusion | flops 25165824 | bytes 4393984 | tf_op jit(solution)/shard_map/dot_general | solution.py:144
  348.3 6.1 %all-to-all-start.2 = ((f32[16,6,8]{1,2,0:T(8,128)}), f32[16,6,8]{1,2,0:T(8,128)S(1)}, u32[]{:S(2)}, u32[]{:S(2)}) async-start(f32[16,6,8]{1,2,0:T(8,128)} %copy.454), calls=%async_computation.2 | async-start | bytes 131072 | tf_op jit(solution)/shard_map/all_to_all | solution.py:49
  354.4 6.6 %fusion.12 = f32[16,8,6]{2,1,0:T(8,128)} fusion(bf16[16384,128]{0,1:T(8,128)(2,1)} %fusion.2, bf16[16384,128]{0,1:T(8,128)(2,1)} %copy-done.7, bf16[6,16384]{1,0:T(8,128)(2,1)S(1)} %stack.144, bf16[3,128,128]{2,1,0:T(8,128)(2,1)S(1)} %copy-done.15), kind=kOutput, calls=%fused_computation.22 | convolution fusion | flops 572522496 | bytes 8686592 | tf_op jit(solution)/shard_map/dot_general | solution.py:144
  361.0 4.7 %convolution_bitcast_fusion.4 = f32[1,16,8,128]{3,2,0,1:T(8,128)S(1)} fusion(bf16[16384,128]{0,1:T(8,128)(2,1)} %fusion.2, bf16[16384,128]{0,1:T(8,128)(2,1)} %copy-done.7), kind=kOutput, calls=%fused_computation.25 | convolution fusion | flops 536870912 | bytes 8454144 | tf_op jit(solution)/shard_map/dot_general | solution.py:144
  365.7 5.8 %all-to-all-start = ((f32[16,8,6]{2,1,0:T(8,128)}), f32[16,8,6]{2,1,0:T(8,128)S(1)}, u32[]{:S(2)}, u32[]{:S(2)}) async-start(f32[16,8,6]{2,1,0:T(8,128)} %fusion.12), calls=%async_computation | async-start | bytes 131072 | tf_op jit(solution)/shard_map/all_to_all | solution.py:49
  372.2 5.1 %all-to-all-done = f32[16,8,6]{2,1,0:T(8,128)S(1)} async-done(((f32[16,8,6]{2,1,0:T(8,128)}), f32[16,8,6]{2,1,0:T(8,128)S(1)}, u32[]{:S(2)}, u32[]{:S(2)}) %all-to-all-start) | async-done | bytes 3104 | tf_op jit(solution)/shard_map/all_to_all | solution.py:49
  381.4 6.5 %all-to-all-done.1 = f32[16,3,8,128]{3,2,1,0:T(8,128)S(1)} async-done(((f32[16,3,8,128]{3,2,1,0:T(8,128)}), f32[16,3,8,128]{3,2,1,0:T(8,128)S(1)}, u32[]{:S(2)}, u32[]{:S(2)}) %all-to-all-start.1) | async-done | bytes 196640 | tf_op jit(solution)/shard_map/all_to_all | solution.py:49
  388.0 17.5 %all_to_all.21 = f32[16,1,3168]{2,1,0:T(1,128)S(1)} all-to-all(f32[16,1,3168]{2,1,0:T(1,128)S(1)} %broadcast_in_dim.2), channel_id=1, replica_groups=mesh['patch_0'=8,'patch_1'=2,'sub_0'=2,'sub_1'=4,'sub_2'=2] {'patch_0','..., dimensions={0} | all-to-all | bytes 405504 | tf_op jit(solution)/shard_map/all_to_all | solution.py:55
  406.1 19.9 %all_gather.3 = f32[128,396]{1,0:T(8,128)S(1)} all-gather(f32[8,396]{1,0:T(8,128)S(1)} %pad_maximum_fusion.7), channel_id=1, replica_groups=mesh['patch_0'=8,'patch_1'=2,'sub_0'=2,'sub_1'=4,'sub_2'=2] {'sub_0','su..., dimensions={0}, use_global_device_ids=true | all-gather | bytes 215424 | tf_op jit(solution)/shard_map/all_gather | solution.py:76
  (253 shorter events, 148.1 us)
Async XLA Ops:
  1.7 11.6 %collective-permute-start = (f32[3,1,2048]{2,1,0:T(1,128)S(1)}, f32[3,1,2048]{2,1,0:T(1,128)S(1)}, u32[]{:S(2)}, u32[]{:S(2)}) collective-permute-start(f32[3,1,2048]{2,1,0:T(1,128)S(1)} %get-tuple-element.221), channel_id=1, source_target_pairs={{0,16},{16,32},{32,48},{48,64},{64,80},{80,96},{96,112},{112,128},... | collective-permute-start | bytes 73736 | tf_op jit(solution)/shard_map/ppermute | solution.py:32
  5.4 8.0 %collective-permute-start.1 = (f32[3,1,2048]{2,1,0:T(1,128)S(1)}, f32[3,1,2048]{2,1,0:T(1,128)S(1)}, u32[]{:S(2)}, u32[]{:S(2)}) collective-permute-start(f32[3,1,2048]{2,1,0:T(1,128)S(1)} %get-tuple-element.222), channel_id=1, source_target_pairs={{16,0},{32,16},{48,32},{64,48},{80,64},{96,80},{112,96},{128,112},... | collective-permute-start | bytes 73736 | tf_op jit(solution)/shard_map/ppermute | solution.py:34
  14.5 4.6 %collective-permute-start.3 = (f32[3,10,1]{2,1,0:T(8,128)S(1)}, f32[3,10,1]{2,1,0:T(8,128)S(1)}, u32[]{:S(2)}, u32[]{:S(2)}) collective-permute-start(f32[3,10,1]{2,1,0:T(8,128)S(1)} %get-tuple-element.207), channel_id=1, source_target_pairs={{1,0},{2,1},{3,2},{4,3},{5,4},{6,5},{7,6},{8,7},{9,8},{10,9},{11,1... | collective-permute-start | bytes 368 | tf_op jit(solution)/shard_map/ppermute | solution.py:34
  15.4 3.6 collective-permute-start.2
  34.1 10.6 %collective-permute-start.4 = (f32[6,1,2048]{2,1,0:T(1,128)S(1)}, f32[6,1,2048]{2,1,0:T(1,128)S(1)}, u32[]{:S(2)}, u32[]{:S(2)}) collective-permute-start(f32[6,1,2048]{2,1,0:T(1,128)S(1)} %get-tuple-element.205), channel_id=1, source_target_pairs={{0,16},{16,32},{32,48},{48,64},{64,80},{80,96},{96,112},{112,128},... | collective-permute-start | bytes 147464 | tf_op jit(solution)/shard_map/ppermute | solution.py:32
  34.2 10.5 %collective-permute-start.5 = (f32[6,1,2048]{2,1,0:T(1,128)S(1)}, f32[6,1,2048]{2,1,0:T(1,128)S(1)}, u32[]{:S(2)}, u32[]{:S(2)}) collective-permute-start(f32[6,1,2048]{2,1,0:T(1,128)S(1)} %get-tuple-element.206), channel_id=1, source_target_pairs={{16,0},{32,16},{48,32},{64,48},{80,64},{96,80},{112,96},{128,112},... | collective-permute-start | bytes 147464 | tf_op jit(solution)/shard_map/ppermute | solution.py:34
  39.3 10.9 %collective-permute-start.8 = (s32[1,2048]{1,0:T(1,128)S(1)}, s32[1,2048]{1,0:T(1,128)S(1)}, u32[]{:S(2)}, u32[]{:S(2)}) collective-permute-start(s32[1,2048]{1,0:T(1,128)S(1)} %get-tuple-element.247), channel_id=1, source_target_pairs={{0,16},{16,32},{32,48},{48,64},{64,80},{80,96},{96,112},{112,128},... | collective-permute-start | bytes 24584 | tf_op jit(solution)/shard_map/ppermute | solution.py:32
  39.4 10.8 %collective-permute-start.9 = (s32[1,2048]{1,0:T(1,128)S(1)}, s32[1,2048]{1,0:T(1,128)S(1)}, u32[]{:S(2)}, u32[]{:S(2)}) collective-permute-start(s32[1,2048]{1,0:T(1,128)S(1)} %get-tuple-element.248), channel_id=1, source_target_pairs={{16,0},{32,16},{48,32},{64,48},{80,64},{96,80},{112,96},{128,112},... | collective-permute-start | bytes 24584 | tf_op jit(solution)/shard_map/ppermute | solution.py:34
  45.0 6.1 %collective-permute-start.7 = (f32[6,10,1]{2,1,0:T(8,128)S(1)}, f32[6,10,1]{2,1,0:T(8,128)S(1)}, u32[]{:S(2)}, u32[]{:S(2)}) collective-permute-start(f32[6,10,1]{2,1,0:T(8,128)S(1)} %get-tuple-element.151), channel_id=1, source_target_pairs={{1,0},{2,1},{3,2},{4,3},{5,4},{6,5},{7,6},{8,7},{9,8},{10,9},{11,1... | collective-permute-start | bytes 728 | tf_op jit(solution)/shard_map/ppermute | solution.py:34
  52.5 12.1 %collective-permute-start.12 = (f32[3,2,2048]{2,1,0:T(2,128)S(1)}, f32[3,2,2048]{2,1,0:T(2,128)S(1)}, u32[]{:S(2)}, u32[]{:S(2)}) collective-permute-start(f32[3,2,2048]{2,1,0:T(2,128)S(1)} %get-tuple-element.219), channel_id=1, source_target_pairs={{0,16},{16,32},{32,48},{48,64},{64,80},{80,96},{96,112},{112,128},... | collective-permute-start | bytes 147464 | tf_op jit(solution)/shard_map/ppermute | solution.py:32
  52.6 12.0 %collective-permute-start.13 = (f32[3,2,2048]{2,1,0:T(2,128)S(1)}, f32[3,2,2048]{2,1,0:T(2,128)S(1)}, u32[]{:S(2)}, u32[]{:S(2)}) collective-permute-start(f32[3,2,2048]{2,1,0:T(2,128)S(1)} %get-tuple-element.220), channel_id=1, source_target_pairs={{16,0},{32,16},{48,32},{64,48},{80,64},{96,80},{112,96},{128,112},... | collective-permute-start | bytes 147464 | tf_op jit(solution)/shard_map/ppermute | solution.py:34
  57.7 6.3 %collective-permute-start.11 = (s32[10,1]{1,0:T(8,128)S(1)}, s32[10,1]{1,0:T(8,128)S(1)}, u32[]{:S(2)}, u32[]{:S(2)}) collective-permute-start(s32[10,1]{1,0:T(8,128)S(1)} %get-tuple-element.231), channel_id=1, source_target_pairs={{1,0},{2,1},{3,2},{4,3},{5,4},{6,5},{7,6},{8,7},{9,8},{10,9},{11,1... | collective-permute-start | bytes 128 | tf_op jit(solution)/shard_map/ppermute | solution.py:34
  64.7 9.6 %collective-permute-start.15 = (f32[3,12,2]{2,1,0:T(8,128)S(1)}, f32[3,12,2]{2,1,0:T(8,128)S(1)}, u32[]{:S(2)}, u32[]{:S(2)}) collective-permute-start(f32[3,12,2]{2,1,0:T(8,128)S(1)} %get-tuple-element.203), channel_id=1, source_target_pairs={{1,0},{2,1},{3,2},{4,3},{5,4},{6,5},{7,6},{8,7},{9,8},{10,9},{11,1... | collective-permute-start | bytes 872 | tf_op jit(solution)/shard_map/ppermute | solution.py:34
  68.8 5.6 %collective-permute-start.14 = (f32[3,12,2]{2,1,0:T(8,128)S(1)}, f32[3,12,2]{2,1,0:T(8,128)S(1)}, u32[]{:S(2)}, u32[]{:S(2)}) collective-permute-start(f32[3,12,2]{2,1,0:T(8,128)S(1)} %get-tuple-element.204), channel_id=1, source_target_pairs={{0,1},{1,2},{2,3},{3,4},{4,5},{5,6},{6,7},{7,8},{8,9},{9,10},{10,1... | collective-permute-start | bytes 872 | tf_op jit(solution)/shard_map/ppermute | solution.py:32
  119.4 6.6 %collective-permute-start.16 = (f32[3,2,2048]{2,1,0:T(2,128)S(1)}, f32[3,2,2048]{2,1,0:T(2,128)S(1)}, u32[]{:S(2)}, u32[]{:S(2)}) collective-permute-start(f32[3,2,2048]{2,1,0:T(2,128)S(1)} %get-tuple-element.217), channel_id=1, source_target_pairs={{0,16},{16,32},{32,48},{48,64},{64,80},{80,96},{96,112},{112,128},... | collective-permute-start | bytes 147464 | tf_op jit(solution)/shard_map/ppermute | solution.py:32
  122.1 5.0 %collective-permute-start.17 = (f32[3,2,2048]{2,1,0:T(2,128)S(1)}, f32[3,2,2048]{2,1,0:T(2,128)S(1)}, u32[]{:S(2)}, u32[]{:S(2)}) collective-permute-start(f32[3,2,2048]{2,1,0:T(2,128)S(1)} %get-tuple-element.218), channel_id=1, source_target_pairs={{16,0},{32,16},{48,32},{64,48},{80,64},{96,80},{112,96},{128,112},... | collective-permute-start | bytes 147464 | tf_op jit(solution)/shard_map/ppermute | solution.py:34
  127.3 4.3 %collective-permute-start.19 = (f32[3,12,2]{2,1,0:T(8,128)S(1)}, f32[3,12,2]{2,1,0:T(8,128)S(1)}, u32[]{:S(2)}, u32[]{:S(2)}) collective-permute-start(f32[3,12,2]{2,1,0:T(8,128)S(1)} %get-tuple-element.201), channel_id=1, source_target_pairs={{1,0},{2,1},{3,2},{4,3},{5,4},{6,5},{7,6},{8,7},{9,8},{10,9},{11,1... | collective-permute-start | bytes 872 | tf_op jit(solution)/shard_map/ppermute | solution.py:34
  185.9 6.6 %collective-permute-start.20 = (f32[3,2,2048]{2,1,0:T(2,128)S(1)}, f32[3,2,2048]{2,1,0:T(2,128)S(1)}, u32[]{:S(2)}, u32[]{:S(2)}) collective-permute-start(f32[3,2,2048]{2,1,0:T(2,128)S(1)} %get-tuple-element.215), channel_id=1, source_target_pairs={{0,16},{16,32},{32,48},{48,64},{64,80},{80,96},{96,112},{112,128},... | collective-permute-start | bytes 147464 | tf_op jit(solution)/shard_map/ppermute | solution.py:32
  189.3 4.6 %collective-permute-start.21 = (f32[3,2,2048]{2,1,0:T(2,128)S(1)}, f32[3,2,2048]{2,1,0:T(2,128)S(1)}, u32[]{:S(2)}, u32[]{:S(2)}) collective-permute-start(f32[3,2,2048]{2,1,0:T(2,128)S(1)} %get-tuple-element.216), channel_id=1, source_target_pairs={{16,0},{32,16},{48,32},{64,48},{80,64},{96,80},{112,96},{128,112},... | collective-permute-start | bytes 147464 | tf_op jit(solution)/shard_map/ppermute | solution.py:34
  194.1 4.9 %collective-permute-start.23 = (f32[3,12,2]{2,1,0:T(8,128)S(1)}, f32[3,12,2]{2,1,0:T(8,128)S(1)}, u32[]{:S(2)}, u32[]{:S(2)}) collective-permute-start(f32[3,12,2]{2,1,0:T(8,128)S(1)} %get-tuple-element.199), channel_id=1, source_target_pairs={{1,0},{2,1},{3,2},{4,3},{5,4},{6,5},{7,6},{8,7},{9,8},{10,9},{11,1... | collective-permute-start | bytes 872 | tf_op jit(solution)/shard_map/ppermute | solution.py:34
  195.8 3.1 collective-permute-start.22
  250.5 6.6 %collective-permute-start.24 = (f32[3,2,2048]{2,1,0:T(2,128)S(1)}, f32[3,2,2048]{2,1,0:T(2,128)S(1)}, u32[]{:S(2)}, u32[]{:S(2)}) collective-permute-start(f32[3,2,2048]{2,1,0:T(2,128)S(1)} %get-tuple-element.213), channel_id=1, source_target_pairs={{0,16},{16,32},{32,48},{48,64},{64,80},{80,96},{96,112},{112,128},... | collective-permute-start | bytes 147464 | tf_op jit(solution)/shard_map/ppermute | solution.py:32
  253.8 4.6 %collective-permute-start.25 = (f32[3,2,2048]{2,1,0:T(2,128)S(1)}, f32[3,2,2048]{2,1,0:T(2,128)S(1)}, u32[]{:S(2)}, u32[]{:S(2)}) collective-permute-start(f32[3,2,2048]{2,1,0:T(2,128)S(1)} %get-tuple-element.214), channel_id=1, source_target_pairs={{16,0},{32,16},{48,32},{64,48},{80,64},{96,80},{112,96},{128,112},... | collective-permute-start | bytes 147464 | tf_op jit(solution)/shard_map/ppermute | solution.py:34
  258.6 4.8 %collective-permute-start.27 = (f32[3,12,2]{2,1,0:T(8,128)S(1)}, f32[3,12,2]{2,1,0:T(8,128)S(1)}, u32[]{:S(2)}, u32[]{:S(2)}) collective-permute-start(f32[3,12,2]{2,1,0:T(8,128)S(1)} %get-tuple-element.197), channel_id=1, source_target_pairs={{1,0},{2,1},{3,2},{4,3},{5,4},{6,5},{7,6},{8,7},{9,8},{10,9},{11,1... | collective-permute-start | bytes 872 | tf_op jit(solution)/shard_map/ppermute | solution.py:34
  260.2 3.1 collective-permute-start.26
  315.8 6.4 %collective-permute-start.28 = (f32[3,1,2048]{2,1,0:T(1,128)S(1)}, f32[3,1,2048]{2,1,0:T(1,128)S(1)}, u32[]{:S(2)}, u32[]{:S(2)}) collective-permute-start(f32[3,1,2048]{2,1,0:T(1,128)S(1)} %get-tuple-element.211), channel_id=1, source_target_pairs={{0,16},{16,32},{32,48},{48,64},{64,80},{80,96},{96,112},{112,128},... | collective-permute-start | bytes 73736 | tf_op jit(solution)/shard_map/ppermute | solution.py:32
  319.1 4.2 collective-permute-start.29
  323.5 4.9 %collective-permute-start.31 = (f32[3,10,1]{2,1,0:T(8,128)S(1)}, f32[3,10,1]{2,1,0:T(8,128)S(1)}, u32[]{:S(2)}, u32[]{:S(2)}) collective-permute-start(f32[3,10,1]{2,1,0:T(8,128)S(1)} %get-tuple-element.195), channel_id=1, source_target_pairs={{1,0},{2,1},{3,2},{4,3},{5,4},{6,5},{7,6},{8,7},{9,8},{10,9},{11,1... | collective-permute-start | bytes 368 | tf_op jit(solution)/shard_map/ppermute | solution.py:34
  325.3 3.1 collective-permute-start.30
  348.3 17.4 %all-to-all-start.2 = ((f32[16,6,8]{1,2,0:T(8,128)}), f32[16,6,8]{1,2,0:T(8,128)S(1)}, u32[]{:S(2)}, u32[]{:S(2)}) async-start(f32[16,6,8]{1,2,0:T(8,128)} %copy.454), calls=%async_computation.2 | async-start | bytes 131072 | tf_op jit(solution)/shard_map/all_to_all | solution.py:49
  365.7 11.6 %all-to-all-start = ((f32[16,8,6]{2,1,0:T(8,128)}), f32[16,8,6]{2,1,0:T(8,128)S(1)}, u32[]{:S(2)}, u32[]{:S(2)}) async-start(f32[16,8,6]{2,1,0:T(8,128)} %fusion.12), calls=%async_computation | async-start | bytes 131072 | tf_op jit(solution)/shard_map/all_to_all | solution.py:49
  377.3 10.5 %all-to-all-start.1 = ((f32[16,3,8,128]{3,2,1,0:T(8,128)}), f32[16,3,8,128]{3,2,1,0:T(8,128)S(1)}, u32[]{:S(2)}, u32[]{:S(2)}) async-start(f32[16,3,8,128]{3,2,1,0:T(8,128)} %maximum_bitcast_fusion), calls=%async_computation.1 | async-start | bytes 393216 | tf_op jit(solution)/shard_map/all_to_all | solution.py:49
  (25 other events, 529.6 us)
where the time goes:
time: 434 us; the launch traced here: 429 us
  blocking collectives  207 us (48%)
  starting transfers between devices  92.2 us (21%)
  matrix products  38.8 us (9%)
  waiting for transfers between devices  29.8 us (7%)
  other arithmetic  24.1 us (6%)
  local copies, waits for them, and re-layouts  21.2 us (5%)
  between operations  15.8 us (4%)
    psum x20, blocking collectives, by_axis(): return functools.reduce(lax.psum, axes, value)  169 us
    ppermute x16, starting transfers between devices, padded_2(): lax.ppermute(head, axis, [((i + 1) % count, i) for i in range(count)])  51.1 us
    ppermute x16, starting transfers between devices, padded_2(): lax.ppermute(tail, axis, [(i, (i + 1) % count) for i in range(count)])  25.5 us
    all_gather x1, blocking collectives, turned_gather(): filled, at, done = (lax.all_gather(both, axis, axis=0, tiled=True), 0, [])  19.9 us
    dot_general x5, matrix products, outer_product(): lax.dot_general(left, right, (((1,), (1,)), ((), ())), preferred_element_...  18.7 us
    all_to_all x1, blocking collectives, sent_to_all(): lax.all_to_all(jnp.broadcast_to(value[None], (size, *value.shape)), axis,...  17.5 us
    all_to_all x3, starting transfers between devices, sent_and_summed(): pieces = lax.all_to_all(split_up(value, dim, size), axis, 0, 0, tiled=True)  15.6 us
    ppermute x16, waiting for transfers between devices, padded_2(): lax.ppermute(head, axis, [((i + 1) % count, i) for i in range(count)])  12 us
  transfers between devices with their start and end apart: 35, of which 18 were waited for; matrix products, arithmetic and copies ran while one was open for 5% of the time, Pallas kernels for 0%

commit v1 on v0

--- a/solution.py
+++ b/solution.py
@@ -3,13 +3,14 @@
 import jax
 import jax.numpy as jnp
 from jax import lax
-from jax.sharding import Mesh
+from jax.experimental import pallas as pl
+from jax.experimental.pallas import tpu as pltpu
 from jax.sharding import PartitionSpec as P
 
 ITERS = 4
-PATCH_SUB = ("patch_0", "patch_1", "sub_0", "sub_1", "sub_2")
-PATCH = ("patch_0", "patch_1")
-SUB = ("sub_0", "sub_1", "sub_2")
+PATCH_SUB = ("patch", "sub")
+PATCH = "patch"
+SUB = "sub"
 
 
 BASIS_VALUE = (0.125, 0.75, 0.125)
@@ -19,7 +20,7 @@
 
 
 def by_axis(value, axes):
-    return functools.reduce(lax.psum, axes, value)
+    return lax.psum(value, axes)
 
 
 def padded_2(cells, sides, width):
@@ -183,7 +184,7 @@
     )
 
 
-def per_device(displacement, load, foundation, layup, layup_stiffness, w_first, w_mid, w_last):
+def careful(displacement, load, foundation, layup, layup_stiffness, w_first, w_mid, w_last):
     layup_count = layup_stiffness.shape[0]
 
     def coefficients(layup_ids):
@@ -237,23 +238,572 @@
     return (residual, adjoint, totals[0], totals[1], totals[2])
 
 
+ROWS = 24
+SEGS = 24
+LANES = 128
+OWN = 8
+TILES = 16
+STEP = 512
+TRUST = 400.0
+MESH = pl.DeviceIdType.MESH
+PAIRS = [(a, b) for a in range(6) for b in range(a, 6)]
+SPOT = {pair: k for k, pair in enumerate(PAIRS)}
+
+
+def flat(ref):
+    lead, mid, lanes = ref.shape
+    return ref.reshape(lead * mid, lanes)
+
+
+def column(ref, fields, field, row, segment):
+    return flat(ref).at[pl.ds((row * fields + field) * SEGS + segment, 8, stride=fields * SEGS), :]
+
+
+def lane_of():
+    return lax.broadcasted_iota(jnp.int32, (SEGS, LANES), 1)
+
+
+def after(field, lane):
+    turned = pltpu.roll(field, LANES - 1, 1)
+    return jnp.where(lane == LANES - 1, pltpu.roll(turned, SEGS - 1, 0), turned)
+
+
+def before(field, lane):
+    turned = pltpu.roll(field, 1, 1)
+    return jnp.where(lane == 0, pltpu.roll(turned, 1, 0), turned)
+
+
+def along_columns(read, y_ref, first, last):
+    lane = lane_of()
+
+    def body(e, carry):
+        u, v, w = read(e)
+        at = e * 7
+        for k, field in enumerate((u, v, w)):
+            ahead, behind = after(field, lane), before(field, lane)
+            both = ahead + behind
+            y_ref[at + 2 * k] = 0.75 * field + 0.125 * both
+            y_ref[at + 2 * k + 1] = 0.5 * (ahead - behind)
+            if k == 2:
+                y_ref[at + 6] = both - 2.0 * field
+        return carry
+
+    lax.fori_loop(first, last, body, 0, unroll=2)
+
+
+def strains_at(y_ref, e):
+    at = e * 7
+
+    def three(k):
+        return y_ref[at - 7 + k], y_ref[at + k], y_ref[at + 7 + k]
+
+    def value(k):
+        m, c, p = three(k)
+        return 0.75 * c + 0.125 * (p + m)
+
+    def slope(k):
+        return 0.5 * (y_ref[at + 7 + k] - y_ref[at - 7 + k])
+
+    m, c, p = three(4)
+    pair = p + m
+    return [
+        slope(0),
+        value(3) + HOOP_CURVATURE * (0.75 * c + 0.125 * pair),
+        value(1) + slope(2),
+        2.0 * c - pair,
+        -value(6),
+        y_ref[at - 7 + 5] - y_ref[at + 7 + 5],
+    ]
+
+
+def laminate(c_ref, e, strain):
+    at = e * 21
+    total = [None] * 6
+    for (a, b), k in SPOT.items():
+        c = c_ref[at + k]
+        term = c * strain[b]
+        total[a] = term if total[a] is None else total[a] + term
+        if a != b:
+            term = c * strain[a]
+            total[b] = term if total[b] is None else total[b] + term
+    return total
+
+
+def forces_at(s_ref, e, lane):
+    at = e * 6
+
+    def three(k):
+        return s_ref[at - 6 + k], s_ref[at + k], s_ref[at + 6 + k]
+
+    def value(k):
+        m, c, p = three(k)
+        return 0.75 * c + 0.125 * (p + m)
+
+    def slope(k):
+        return 0.5 * (s_ref[at - 6 + k] - s_ref[at + 6 + k])
+
+    def spread(here, behind, ahead):
+        return here + before(behind, lane) + after(ahead, lane)
+
+    a, b = slope(0), value(2)
+    force_u = spread(0.75 * a, 0.125 * a + 0.5 * b, 0.125 * a - 0.5 * b)
+    a, b = slope(2), value(1)
+    force_v = spread(0.75 * a, 0.125 * a + 0.5 * b, 0.125 * a - 0.5 * b)
+    m, c, p = three(3)
+    a = HOOP_CURVATURE * b - ((m + p) - 2.0 * c)
+    d = value(4)
+    half = slope(5)
+    base = 0.125 * a - d
+    force_w = spread(0.75 * a + 2.0 * d, base - half, base + half)
+    return force_u, force_v, force_w
+
+
+def fused(
+    disp, load, found, lay, stiff, w1, wm, wl,
+    res_o, adj_o, gf_o, gm_o, gl_o, trust_o,
+    dsp, aux, lod, edge_a, edge_c, got_a, got_c, y_ref, s_ref, c_ref, x_ref, l_ref, u_ref, h_ref,
+    v0, v1, v2, v3, wmt, acc_m, acc_s,
+    d_out, d_in, d_mid, d_in2, e_out, e_in, e_mid, e_in2, e_end, e_in3,
+    a_s, a_r, c_s, c_r, d1_s, d1_r, d2_s, d2_r, e1_s, e1_r, e2_s, e2_r, e3_s, e3_r,
+):
+    me_p, me_s = lax.axis_index("patch"), lax.axis_index("sub")
+    count_p, count_s = lax.axis_size("patch"), lax.axis_size("sub")
+
+    def place(dp, ds):
+        return {"patch": lax.rem(me_p + dp, count_p), "sub": lax.rem(me_s + ds, count_s)}
+
+    up, down = count_p - 1, 1
+    left, right = count_s - 1, 1
+    greeted = [(0, k) for k in range(1, count_s)] + [(k, 0) for k in range(1, count_p)]
+    greeted += [(a, b) for a in (up, down) for b in (left, right)]
+    barrier = pltpu.get_barrier_semaphore()
+    for dp, ds in greeted:
+        pl.semaphore_signal(barrier, inc=1, device_id=place(dp, ds), device_id_type=MESH)
+
+    for t in range(TILES):
+        cut = pl.ds(t * LANES, LANES)
+        for f in range(3):
+            column(dsp, 3, f, OWN, 8 + t)[...] = disp[f, :, cut]
+    ends = ((0, pl.ds(0, LANES)), (1, pl.ds((TILES - 1) * LANES, LANES)))
+    for side, cut in ends:
+        for f in range(3):
+            edge_a[side, f] = disp[f, :, cut]
+            edge_a[side, 3 + f] = found[f, :, cut]
+        edge_a[side, 6] = lay[:, cut].astype(jnp.float32)
+
+    pl.semaphore_wait(barrier, len(greeted))
+
+    def send(src, dst, sent, received, to):
+        return pltpu.make_async_remote_copy(
+            src_ref=src, dst_ref=dst, send_sem=sent, recv_sem=received, device_id=to, device_id_type=MESH
+        )
+
+    def rows_to(ref, fields, n, sent, received, first):
+        own = pl.ds(OWN, TILES)
+        below = send(
+            ref.at[pl.ds((16 - n) * fields, n * fields), own, :],
+            ref.at[pl.ds((8 - n) * fields, n * fields), own, :],
+            sent.at[first], received.at[first], place(down, 0),
+        )
+        above = send(
+            ref.at[pl.ds(8 * fields, n * fields), own, :],
+            ref.at[pl.ds(16 * fields, n * fields), own, :],
+            sent.at[first + 1], received.at[first + 1], place(up, 0),
+        )
+        return [below, above]
+
+    heading = ((0, right, 1), (0, left, 0), (down, right, 1), (down, left, 0), (up, right, 1), (up, left, 0))
+
+    def edges_to(edge, got, sent, received, first):
+        return [
+            send(edge.at[side], got.at[k], sent.at[first + k], received.at[first + k], place(dp, ds))
+            for k, (dp, ds, side) in enumerate(heading)
+        ]
+
+    def start(copies):
+        for copy in copies:
+            copy.start()
+
+    landing = ((7, 8), (0, 8), (7, 0), (0, 0), (7, 16), (0, 16))
+
+    first_a = rows_to(dsp, 3, 2, a_s, a_r, 0) + edges_to(edge_a, got_a, a_s, a_r, 2)
+    start(first_a)
+    for t in range(TILES):
+        cut = pl.ds(t * LANES, LANES)
+        for f in range(3):
+            column(aux, 4, f, OWN, 8 + t)[...] = found[f, :, cut]
+        column(aux, 4, 3, OWN, 8 + t)[...] = lay[:, cut].astype(jnp.float32)
+    second_a = rows_to(aux, 4, 6, a_s, a_r, 8)
+    start(second_a)
+    for t in range(TILES):
+        cut = pl.ds(t * LANES, LANES)
+        for f in range(3):
+            column(lod, 3, f, 0, 8 + t)[...] = load[f, :, cut]
+    for k in range(3):
+        wmt[k] = wm[k].T
+
+    for copy in first_a:
+        copy.wait()
+    for k, (segment, row) in enumerate(landing):
+        for f in range(3):
+            column(dsp, 3, f, row, segment)[...] = got_a[k, f]
+            column(aux, 4, f, row, segment)[...] = got_a[k, 3 + f]
+        column(aux, 4, 3, row, segment)[...] = got_a[k, 6]
+
+    lane = lane_of()
+    along_columns(lambda e: [dsp[e * 3 + f] for f in range(3)], y_ref, 6, 18)
+
+    def strain_row(r, carry):
+        e = r + 7
+        strain = strains_at(y_ref, e)
+        for k in range(6):
+            s_ref[e * 6 + k] = strain[k]
+            flat(x_ref)[pl.ds(r * (SEGS * 8) + k, SEGS, stride=8), :] = strain[k]
+        return carry
+
+    lax.fori_loop(0, 10, strain_row, 0)
+    tile_lane = lax.broadcasted_iota(jnp.int32, (8, LANES), 1)
+    for r in range(10):
+        x_ref[10 * SEGS + 8 + r] = jnp.where(tile_lane < 64, x_ref[r * SEGS], x_ref[r * SEGS + 7])
+    for r in range(10, 16):
+        x_ref[10 * SEGS + 8 + r] = jnp.zeros((8, LANES), jnp.float32)
+
+    def operand(ref, r, c):
+        at = r * SEGS + 8 + c * (STEP // LANES)
+        tiles = [ref[at + q] for q in range(STEP // LANES)]
+        return jnp.concatenate(tiles, axis=1)[:6].astype(jnp.bfloat16)
+
+    def learn_row(r, carry):
+        slot = jnp.where((r >= 1) & (r <= 8), r - 1, 8) * 4
+        for c in range(2048 // STEP):
+            cut = pl.ds(c * STEP, STEP)
+            hidden = jnp.tanh(
+                jnp.dot(w1[...], operand(x_ref, r, c), preferred_element_type=jnp.float32)
+            ).astype(jnp.bfloat16)
+            h_ref[slot, :, cut] = hidden
+            for k in range(3):
+                hidden = jnp.tanh(
+                    jnp.dot(wm[k], hidden, preferred_element_type=jnp.float32)
+                ).astype(jnp.bfloat16)
+                h_ref[slot + k + 1, :, cut] = hidden
+            out = jnp.dot(wl[...], hidden, preferred_element_type=jnp.float32)
+            at = r * SEGS + 8 + c * (STEP // LANES)
+            for q in range(STEP // LANES):
+                l_ref[at + q, 0:6, :] = out[:, q * LANES : (q + 1) * LANES]
+        return carry
+
+    lax.fori_loop(0, 11, learn_row, 0)
+    for r in range(10):
+        beside = l_ref[10 * SEGS + 8 + r]
+        l_ref[r * SEGS] = beside
+        l_ref[r * SEGS + 7] = beside
+
+    for copy in second_a:
+        copy.wait()
+
+    def choose_row(e, carry):
+        ids = aux[e * 4 + 3].astype(jnp.int32)
+        low, middle, high = (ids & 1) == 1, (ids & 2) == 2, (ids & 4) == 4
+        for k, (a, b) in enumerate(PAIRS):
+            p = [jnp.where(low, stiff[2 * q + 1, a, b], stiff[2 * q, a, b]) for q in range(4)]
+            c_ref[e * 21 + k] = jnp.where(
+                high, jnp.where(middle, p[3], p[2]), jnp.where(middle, p[1], p[0])
+            )
+        return carry
+
+    lax.fori_loop(7, 17, choose_row, 0)
+
+    def stress_row(r, carry):
+        e = r + 7
+        stress = laminate(c_ref, e, [s_ref[e * 6 + k] for k in range(6)])
+        for k in range(6):
+            s_ref[e * 6 + k] = stress[k] + flat(l_ref)[pl.ds(r * (SEGS * 8) + k, SEGS, stride=8), :]
+        return carry
+
+    lax.fori_loop(0, 10, stress_row, 0)
+
+    def residual_row(e, carry):
+        force = forces_at(s_ref, e, lane)
+        for f in range(3):
+            v0[e * 3 + f] = (
+                force[f] + aux[e * 4 + f] * dsp[e * 3 + f] - lod[(e - 8) * 3 + f]
+            )
+        return carry
+
+    lax.fori_loop(8, 16, residual_row, 0)
+    for side, t in ((0, 0), (1, TILES - 1)):
+        for f in range(3):
+            edge_c[side, f] = column(v0, 3, f, OWN, 8 + t)[...]
+    moves_c = rows_to(v0, 3, 7, c_s, c_r, 0) + edges_to(edge_c, got_c, c_s, c_r, 2)
+    start(moves_c)
+    for t in range(TILES):
+        for f in range(3):
+            res_o[f, :, pl.ds(t * LANES, LANES)] = column(v0, 3, f, OWN, 8 + t)[...]
+    lax.fori_loop(2, 7, choose_row, 0)
+    lax.fori_loop(17, 22, choose_row, 0)
+    for copy in moves_c:
+        copy.wait()
+    for k, (segment, row) in enumerate(landing):
+        for f in range(3):
+            column(v0, 3, f, row, segment)[...] = got_c[k, f]
+
+    def mean(k):
+        total = stiff[0, k, k]
+        for q in range(1, 8):
+            total = total + stiff[q, k, k]
+        return total * 0.125
+
+    half = 1.0 + 8.0 * jnp.maximum(mean(3), mean(4))
+    center = jnp.full((1, LANES), half, jnp.float32)
+    inverse = 1.0 / center
+
+    def apply_stiffness(v, older, out, first, last):
+        along_columns(lambda e: [v[e * 3 + f] for f in range(3)], y_ref, first - 2, last + 2)
+
+        def body(e, carry):
+            stress = laminate(c_ref, e, strains_at(y_ref, e))
+            for k in range(6):
+                s_ref[e * 6 + k] = stress[k]
+            return carry
+
+        lax.fori_loop(first - 1, last + 1, body, 0)
+
+        def finish(e, carry):
+            force = forces_at(s_ref, e, lane)
+            for f in range(3):
+                here = v[e * 3 + f]
+                image = force[f] + aux[e * 4 + f] * here
+                if older is None:
+                    out[e * 3 + f] = inverse * image - here
+                else:
+                    out[e * 3 + f] = (2.0 * inverse) * image - 2.0 * here - older[e * 3 + f]
+            return carry
+
+        lax.fori_loop(first, last, finish, 0)
+
+    apply_stiffness(v0, None, v1, 3, 21)
+    apply_stiffness(v1, v0, v2, 5, 19)
+    apply_stiffness(v2, v1, v3, 7, 17)
+    along_columns(lambda e: [v3[e * 3 + f] for f in range(3)], y_ref, 7, 17)
+
+    def folded(field):
+        return field[8:16] + field[16:24]
+
+    def sums_row(e, totals):
+        strain = strains_at(y_ref, e)
+        stress = laminate(c_ref, e, strain)
+        energy = strain[0] * stress[0]
+        for k in range(1, 6):
+            energy = energy + strain[k] * stress[k]
+        totals = list(totals)
+        for f in range(3):
+            a, b, c, d = v0[e * 3 + f], v1[e * 3 + f], v2[e * 3 + f], v3[e * 3 + f]
+            energy = energy + aux[e * 4 + f] * (d * d)
+            for k, product in enumerate((a * a, a * b, b * b, b * c, c * c, c * d, d * d)):
+                totals[k] = totals[k] + folded(product)
+        totals[7] = totals[7] + folded(energy)
+        return tuple(totals)
+
+    totals = lax.fori_loop(8, 16, sums_row, tuple(jnp.zeros((8, LANES), jnp.float32) for _ in range(8)))
+    d_out[...] = jnp.concatenate([jnp.sum(t, axis=0, keepdims=True) for t in totals], axis=0)
+
+    def shared(source, slots, sent, received, count, mine, spot, piece=None):
+        copies = []
+        for k in range(1, count):
+            to = spot(k)
+            other = lax.rem(mine + k, count)
+            src = source if piece is None else source.at[other]
+            copies.append(send(src, slots.at[mine], sent.at[k], received.at[mine], to))
+        start(copies)
+        own = source if piece is None else source.at[mine]
+        slots[mine] = own[...]
+        for k in range(1, count):
+            other = lax.rem(mine + k, count)
+            src = source if piece is None else source.at[other]
+            send(src, slots.at[other], sent.at[k], received.at[other], spot(k)).wait()
+
+    def summed(slots, count):
+        total = slots[0]
+        for k in range(1, count):
+            total = total + slots[k]
+        return total
+
+    by_sub, by_patch = (lambda k: place(0, k)), (lambda k: place(k, 0))
+    shared(d_out, d_in, d1_s, d1_r, count_s, me_s, by_sub)
+    d_mid[...] = summed(d_in, count_s)
+    shared(d_mid, d_in2, d2_s, d2_r, count_p, me_p, by_patch)
+    everyone = jnp.sum(summed(d_in2, count_p), axis=1, keepdims=True)
+    n = [jnp.broadcast_to(everyone[k : k + 1], (1, LANES)) for k in range(8)]
+    n34 = (2.0 * inverse) * n[7] - 2.0 * n[6] - n[5]
+    m = [n[0], n[1]]
+    for k in (2, 3, 4, 5, 6):
+        m.append(2.0 * n[k] - m[k % 2])
+    m.append(2.0 * n34 - m[1])
+
+    def gram(i, j):
+        return 0.5 * (m[i + j] + m[abs(i - j)])
+
+    def form(x, y):
+        total, size = None, None
+        for i, a in enumerate(x):
+            for j, b in enumerate(y):
+                term = a * b * gram(i, j)
+                total = term if total is None else total + term
+                size = jnp.abs(term) if size is None else size + jnp.abs(term)
+        return total, size / total
+
+    def image_of(x):
+        zero = jnp.zeros((1, LANES), jnp.float32)
+        out = [center * a for a in x] + [zero]
+        for j, a in enumerate(x):
+            if j == 0:
+                out[1] = out[1] + center * a
+            else:
+                out[j + 1] = out[j + 1] + (0.5 * center) * a
+                out[j - 1] = out[j - 1] + (0.5 * center) * a
+        return out
+
+    one = jnp.ones((1, LANES), jnp.float32)
+    zero = jnp.zeros((1, LANES), jnp.float32)
+    rest, way, found_y, norm = [one], [one], [zero] * 4, m[0]
+    worst = one
+    for step in range(ITERS):
+        image = image_of(way)
+        curved, spread = form(way, image)
+        worst = jnp.where(spread <= TRUST, worst, 2.0 * TRUST * one)
+        alpha = norm / curved
+        found_y = [found_y[k] + alpha * way[k] if k < len(way) else found_y[k] for k in range(4)]
+        if step + 1 < ITERS:
+            rest = [(rest[k] if k < len(rest) else zero) - alpha * image[k] for k in range(len(image))]
+            fresh, spread = form(rest, rest)
+            worst = jnp.where(spread <= TRUST, worst, 2.0 * TRUST * one)
+            beta = fresh / norm
+            way = [rest[k] + (beta * way[k] if k < len(way) else zero) for k in range(len(rest))]
+            norm = fresh
+    trust_o[...] = jnp.broadcast_to(worst, (8, LANES))
+
+    def adjoint_row(e, carry):
+        for f in range(3):
+            at = e * 3 + f
+            v0[at] = found_y[0] * v0[at] + found_y[1] * v1[at] + found_y[2] * v2[at] + found_y[3] * v3[at]
+        return carry
+
+    lax.fori_loop(7, 17, adjoint_row, 0)
+    for t in range(TILES):
+        for f in range(3):
+            adj_o[f, :, pl.ds(t * LANES, LANES)] = column(v0, 3, f, OWN, 8 + t)[...]
+    along_columns(lambda e: [v0[e * 3 + f] for f in range(3)], y_ref, 7, 17)
+
+    def upstream_row(e, carry):
+        strain = strains_at(y_ref, e)
+        for k in range(6):
+            flat(u_ref)[pl.ds((e - 8) * (SEGS * 8) + k, SEGS, stride=8), :] = strain[k]
+        return carry
+
+    lax.fori_loop(8, 16, upstream_row, 0)
+
+    acc_m[...] = jnp.zeros_like(acc_m)
+    acc_s[...] = jnp.zeros_like(acc_s)
+    wlt = wl[...].T
+
+    def back_row(r, carry):
+        slot = r * 4
+        for c in range(2048 // STEP):
+            cut = pl.ds(c * STEP, STEP)
+            u = operand(u_ref, r, c)
+            h = h_ref[slot + 3, :, cut]
+            acc_s[0:6] += outer_product(u, h)
+            signal = jnp.dot(wlt, u, preferred_element_type=jnp.float32)
+            d = (signal * (1.0 - jnp.square(h.astype(jnp.float32)))).astype(jnp.bfloat16)
+            for k in range(2, -1, -1):
+                h = h_ref[slot + k, :, cut]
+                acc_m[pl.ds(k * 128, 128)] += outer_product(d, h)
+                signal = jnp.dot(wmt[k], d, preferred_element_type=jnp.float32)
+                d = (signal * (1.0 - jnp.square(h.astype(jnp.float32)))).astype(jnp.bfloat16)
+            acc_s[8:14] += outer_product(operand(x_ref, r + 1, c), d)
+        return carry
+
+    lax.fori_loop(0, 8, back_row, 0)
+
+    whole = jnp.concatenate([acc_m[...], acc_s[...]], axis=0)
+    for k in range(16):
+        e_out[k, 0:25, :] = whole[25 * k : 25 * (k + 1)]
+    shared(e_out, e_in, e1_s, e1_r, count_s, me_s, by_sub, piece=True)
+    e_mid[...] = summed(e_in, count_s)
+    shared(e_mid, e_in2, e2_s, e2_r, count_p, me_p, by_patch)
+    e_end[...] = summed(e_in2, count_p)
+    shared(e_end, e_in3, e3_s, e3_r, count_s, me_s, by_sub)
+    whole = jnp.concatenate([e_in3[k, 0:25, :] for k in range(16)], axis=0)
+    for k in range(3):
+        gm_o[k] = whole[128 * k : 128 * (k + 1)]
+    gl_o[...] = whole[384:390]
+    gf_o[...] = whole[392:400].T[:, 0:6]
+
+
+def per_device(displacement, load, foundation, layup, layup_stiffness, w_first, w_mid, w_last):
+    vmem = pl.BlockSpec(memory_space=pltpu.VMEM)
+    smem = pl.BlockSpec(memory_space=pltpu.SMEM)
+    f32, bf16 = jnp.float32, jnp.bfloat16
+
+    def rows(fields, count=ROWS):
+        return pltpu.VMEM((count * fields, SEGS, LANES), f32)
+
+    dma = pltpu.SemaphoreType.DMA
+    out = pl.pallas_call(
+        fused,
+        out_shape=[
+            jax.ShapeDtypeStruct(displacement.shape, f32),
+            jax.ShapeDtypeStruct(displacement.shape, f32),
+            jax.ShapeDtypeStruct((128, 6), f32),
+            jax.ShapeDtypeStruct((3, 128, 128), f32),
+            jax.ShapeDtypeStruct((6, 128), f32),
+            jax.ShapeDtypeStruct((8, LANES), f32),
+        ],
+        in_specs=[vmem] * 4 + [smem] + [vmem] * 3,
+        out_specs=[vmem] * 6,
+        scratch_shapes=[
+            rows(3), rows(4), rows(3, 8),
+            pltpu.VMEM((2, 7, 8, LANES), f32), pltpu.VMEM((2, 3, 8, LANES), f32),
+            pltpu.VMEM((6, 7, 8, LANES), f32), pltpu.VMEM((6, 3, 8, LANES), f32),
+            rows(7), rows(6), rows(21),
+            pltpu.VMEM((11 * SEGS, 8, LANES), f32),
+            pltpu.VMEM((11 * SEGS, 8, LANES), f32),
+            pltpu.VMEM((8 * SEGS, 8, LANES), f32),
+            pltpu.VMEM((9 * 4, 128, 2048), bf16),
+            rows(3), rows(3), rows(3), rows(3),
+            pltpu.VMEM((3, 128, 128), bf16),
+            pltpu.VMEM((384, 128), f32), pltpu.VMEM((16, 128), f32),
+            pltpu.VMEM((8, LANES), f32), pltpu.VMEM((16, 8, LANES), f32),
+            pltpu.VMEM((8, LANES), f32), pltpu.VMEM((16, 8, LANES), f32),
+            pltpu.VMEM((16, 32, LANES), f32), pltpu.VMEM((16, 32, LANES), f32),
+            pltpu.VMEM((32, LANES), f32), pltpu.VMEM((16, 32, LANES), f32),
+            pltpu.VMEM((32, LANES), f32), pltpu.VMEM((16, 32, LANES), f32),
+            dma((10,)), dma((10,)), dma((8,)), dma((8,)),
+        ] + [dma((16,)) for _ in range(10)],
+        compiler_params=pltpu.CompilerParams(
+            collective_id=0, has_side_effects=True, vmem_limit_bytes=60 << 20
+        ),
+        name="adjoint_step",
+    )(displacement, load, foundation, layup, layup_stiffness, w_first, w_mid, w_last)
+    fast, trust = tuple(out[:5]), out[5][0, 0]
+    operands = (displacement, load, foundation, layup, layup_stiffness, w_first, w_mid, w_last)
+    return lax.cond(trust <= TRUST, lambda: fast, lambda: careful(*operands))
+
+
 def solution(mesh):
-    split = Mesh(
-        mesh.devices.reshape(8, 2, 2, 4, 2), ("patch_0", "patch_1", "sub_0", "sub_1", "sub_2")
-    )
     return jax.shard_map(
         per_device,
-        mesh=split,
+        mesh=mesh,
         in_specs=(
-            P(None, PATCH, SUB),
-            P(None, PATCH, SUB),
-            P(None, PATCH, SUB),
-            P(PATCH, SUB),
+            P(None, "patch", "sub"),
+            P(None, "patch", "sub"),
+            P(None, "patch", "sub"),
+            P("patch", "sub"),
             P(),
             P(),
             P(),
             P(),
         ),
-        out_specs=(P(None, PATCH, SUB), P(None, PATCH, SUB), P(), P(), P()),
+        out_specs=(P(None, "patch", "sub"), P(None, "patch", "sub"), P(), P(), P()),
         check_vma=False,
     )

time: 434 us -> 147 us (0.34); the launches traced: 429 us -> 146 us
  blocking collectives: 207 us -> 0 us
  Pallas kernels: 0 us -> 135 us
  starting transfers between devices: 92.2 us -> 0 us
  matrix products: 38.8 us -> 0 us
  waiting for transfers between devices: 29.8 us -> 0 us
  other arithmetic: 24.1 us -> 0 us
  between operations: 15.8 us -> 1.3 us
  local copies, waits for them, and re-layouts: 21.2 us -> 9.39 us
    psum x20 -> x0, blocking collectives: 169 us -> none  [by_axis(): return functools.reduce(lax.psum, axes, value)]
    pallas_call x0 -> x1, Pallas kernels: none -> 135 us  [per_device(): pl.pallas_call(fused, out_shape=[jax.ShapeDtypeStruct(displacement.shape,...]
    ppermute x32 -> x0, starting transfers between devices: 76.5 us -> none  [the longest x16 51.1 us: padded_2(): lax.ppermute(head, axis, [((i + 1) % count, i) for i in range(count)])]
    dot_general x15 -> x0, matrix products: 38.8 us -> none  [the longest x5 18.7 us: outer_product(): lax.dot_general(left, right, (((1,), (1,)), ((), ())), preferred_element_...]
    all_gather x1 -> x0, blocking collectives: 19.9 us -> none  [turned_gather(): filled, at, done = (lax.all_gather(both, axis, axis=0, tiled=True), 0, [])]
    ppermute x32 -> x0, waiting for transfers between devices: 18.2 us -> none  [the longest x16 12 us: padded_2(): lax.ppermute(head, axis, [((i + 1) % count, i) for i in range(count)])]
    all_to_all x1 -> x0, blocking collectives: 17.5 us -> none  [sent_to_all(): lax.all_to_all(jnp.broadcast_to(value[None], (size, *value.shape)), axis,...]
    all_to_all x3 -> x0, starting transfers between devices: 15.6 us -> none  [sent_and_summed(): pieces = lax.all_to_all(split_up(value, dim, size), axis, 0, 0, tiled=True)]
  transfers between devices with their start and end apart: 35 -> 0, of which waited for: 18 -> 0; matrix products, arithmetic and copies ran while one was open for 5% -> 0% of each run, Pallas kernels for 0% -> 0%
where the time goes in v1:
time: 147 us; the launch traced here: 146 us
  Pallas kernels  135 us (92%)
  local copies, waits for them, and re-layouts  9.39 us (6%)
    pallas_call x1, Pallas kernels, per_device(): pl.pallas_call(fused, out_shape=[jax.ShapeDtypeStruct(displacement.shape,...  135 us
    unnamed x8, local copies, waits for them, and re-layouts  7.3 us

profile of v1, /device:TPU:1, one launch (start us, length us, event | category | flops | bytes accessed | tf_op | source)
XLA Modules:
  0.0 146.4 jit_solution(10943620897000335465)
XLA Ops:
  0.6 1.4 copy.494.stiff
  2.0 1.4 copy.495.w1
  3.4 135.4 %adjoint_step.1 = (f32[3,8,2048]{2,1,0:T(8,128)S(1)}, f32[3,8,2048]{2,1,0:T(8,128)}, f32[128,6]{1,0:T(8,128)}, f32[3,128,128]{2,1,0:T(8,128)}, f32[6,128]{1,0:T(8,128)S(1)}, /*index=5*/f32[8,128]{1,0:T(8,128)}) custom-call(f32[3,8,2048]{2,1,0:T(8,128)} %disp.1, f32[3,8,2048]{2,1,0:T(8,128)} %load.1, f32[3,8,2048]{2,1,0:T(8,128)} %found.1, s32[8,2048]{1,0:T(8,128)} %lay.1, ...), custom_call_target="tpu_custom_call" | custom-call | tf_op jit(solution)/shard_map/adjoint_step/pallas_call | solution.py:752
  138.8 1.2 slice.1661
  140.7 1.1 conditional.1
  140.9 0.9 copy.512
  141.8 0.0 copy-start.22
  141.8 0.7 copy.562
  142.5 1.6 %copy.563 = f32[3,8,2048]{2,1,0:T(8,128)} copy(f32[3,8,2048]{2,1,0:T(8,128)} %get-tuple-element.451) | data formatting | bytes 393216
  144.2 1.6 %copy.564 = f32[3,128,128]{2,1,0:T(8,128)} copy(f32[3,128,128]{2,1,0:T(8,128)} %get-tuple-element.453) | data formatting | bytes 393216
  145.8 0.6 copy.565
  146.4 0.0 copy-done.22
Async XLA Ops:
  141.8 4.5 %copy-start.22 = (f32[128,6]{0,1:T(8,128)}, f32[128,6]{0,1:T(8,128)S(1)}, u32[]{:S(2)}) copy-start(f32[128,6]{0,1:T(8,128)S(1)} %get-tuple-element.452) | copy-start | bytes 9220

commit v2 on v1

--- a/solution.py
+++ b/solution.py
@@ -359,12 +359,14 @@
 
 
 def fused(
-    disp, load, found, lay, stiff, w1, wm, wl,
+    disp, load, found, lay, stiff, w1t, wm, wl,
     res_o, adj_o, gf_o, gm_o, gl_o, trust_o,
-    dsp, aux, lod, edge_a, edge_c, got_a, got_c, y_ref, s_ref, c_ref, x_ref, l_ref, u_ref, h_ref,
+    dsp, aux, ids, lod, edge_a, edge_c, got_a, got_c, y_ref, s_ref, c_ref, x_ref, l_ref, u_ref, h_ref,
     v0, v1, v2, v3, wmt, acc_m, acc_s,
     d_out, d_in, d_mid, d_in2, e_out, e_in, e_mid, e_in2, e_end, e_in3,
+    g_out, g_in, g_mid, g_in2, g_end, g_in3,
     a_s, a_r, c_s, c_r, d1_s, d1_r, d2_s, d2_r, e1_s, e1_r, e2_s, e2_r, e3_s, e3_r,
+    g1_s, g1_r, g2_s, g2_r, g3_s, g3_r,
 ):
     me_p, me_s = lax.axis_index("patch"), lax.axis_index("sub")
     count_p, count_s = lax.axis_size("patch"), lax.axis_size("sub")
@@ -384,6 +386,7 @@
         cut = pl.ds(t * LANES, LANES)
         for f in range(3):
             column(dsp, 3, f, OWN, 8 + t)[...] = disp[f, :, cut]
+        column(ids, 1, 0, OWN, 8 + t)[...] = lay[:, cut].astype(jnp.float32)
     ends = ((0, pl.ds(0, LANES)), (1, pl.ds((TILES - 1) * LANES, LANES)))
     for side, cut in ends:
         for f in range(3):
@@ -398,16 +401,16 @@
             src_ref=src, dst_ref=dst, send_sem=sent, recv_sem=received, device_id=to, device_id_type=MESH
         )
 
-    def rows_to(ref, fields, n, sent, received, first):
-        own = pl.ds(OWN, TILES)
+    def rows_to(ref, fields, near, far, sent, received, first):
+        own, n = pl.ds(OWN, TILES), (far - near) * fields
         below = send(
-            ref.at[pl.ds((16 - n) * fields, n * fields), own, :],
-            ref.at[pl.ds((8 - n) * fields, n * fields), own, :],
+            ref.at[pl.ds((16 - far) * fields, n), own, :],
+            ref.at[pl.ds((8 - far) * fields, n), own, :],
             sent.at[first], received.at[first], place(down, 0),
         )
         above = send(
-            ref.at[pl.ds(8 * fields, n * fields), own, :],
-            ref.at[pl.ds(16 * fields, n * fields), own, :],
+            ref.at[pl.ds((8 + near) * fields, n), own, :],
+            ref.at[pl.ds((16 + near) * fields, n), own, :],
             sent.at[first + 1], received.at[first + 1], place(up, 0),
         )
         return [below, above]
@@ -426,29 +429,42 @@
 
     landing = ((7, 8), (0, 8), (7, 0), (0, 0), (7, 16), (0, 16))
 
-    first_a = rows_to(dsp, 3, 2, a_s, a_r, 0) + edges_to(edge_a, got_a, a_s, a_r, 2)
+    first_a = (
+        rows_to(dsp, 3, 0, 2, a_s, a_r, 0)
+        + edges_to(edge_a, got_a, a_s, a_r, 2)
+        + rows_to(ids, 1, 0, 1, a_s, a_r, 8)
+    )
     start(first_a)
     for t in range(TILES):
         cut = pl.ds(t * LANES, LANES)
         for f in range(3):
-            column(aux, 4, f, OWN, 8 + t)[...] = found[f, :, cut]
-        column(aux, 4, 3, OWN, 8 + t)[...] = lay[:, cut].astype(jnp.float32)
-    second_a = rows_to(aux, 4, 6, a_s, a_r, 8)
-    start(second_a)
-    for t in range(TILES):
-        cut = pl.ds(t * LANES, LANES)
-        for f in range(3):
+            column(aux, 3, f, OWN, 8 + t)[...] = found[f, :, cut]
             column(lod, 3, f, 0, 8 + t)[...] = load[f, :, cut]
     for k in range(3):
         wmt[k] = wm[k].T
+    w1 = w1t[...].T
+    wlt = wl[...].T
+
+    def choose_row(e, carry):
+        kind = ids[e].astype(jnp.int32)
+        low, middle, high = (kind & 1) == 1, (kind & 2) == 2, (kind & 4) == 4
+        for k, (a, b) in enumerate(PAIRS):
+            p = [jnp.where(low, stiff[a, 2 * q + 1, b], stiff[a, 2 * q, b]) for q in range(4)]
+            c_ref[e * 21 + k] = jnp.where(
+                high, jnp.where(middle, p[3], p[2]), jnp.where(middle, p[1], p[0])
+            )
+        return carry
 
     for copy in first_a:
         copy.wait()
     for k, (segment, row) in enumerate(landing):
         for f in range(3):
             column(dsp, 3, f, row, segment)[...] = got_a[k, f]
-            column(aux, 4, f, row, segment)[...] = got_a[k, 3 + f]
-        column(aux, 4, 3, row, segment)[...] = got_a[k, 6]
+            column(aux, 3, f, row, segment)[...] = got_a[k, 3 + f]
+        column(ids, 1, 0, row, segment)[...] = got_a[k, 6]
+    second_a = rows_to(aux, 3, 0, 5, a_s, a_r, 10) + rows_to(ids, 1, 1, 6, a_s, a_r, 12)
+    start(second_a)
+    lax.fori_loop(7, 17, choose_row, 0)
 
     lane = lane_of()
     along_columns(lambda e: [dsp[e * 3 + f] for f in range(3)], y_ref, 6, 18)
@@ -463,55 +479,38 @@
 
     lax.fori_loop(0, 10, strain_row, 0)
     tile_lane = lax.broadcasted_iota(jnp.int32, (8, LANES), 1)
+    beside = 10 * SEGS
+    packed = jnp.zeros((8, LANES), jnp.float32)
     for r in range(10):
-        x_ref[10 * SEGS + 8 + r] = jnp.where(tile_lane < 64, x_ref[r * SEGS], x_ref[r * SEGS + 7])
-    for r in range(10, 16):
-        x_ref[10 * SEGS + 8 + r] = jnp.zeros((8, LANES), jnp.float32)
-
-    def operand(ref, r, c):
-        at = r * SEGS + 8 + c * (STEP // LANES)
-        tiles = [ref[at + q] for q in range(STEP // LANES)]
+        ends_of = jnp.where(tile_lane < 64, x_ref[r * SEGS], x_ref[r * SEGS + 7])
+        turned = pltpu.roll(ends_of, 2 * r + 1, 1)
+        packed = jnp.where((tile_lane == 2 * r) | (tile_lane == 2 * r + 1), turned, packed)
+    x_ref[beside] = packed
+
+    def operand(ref, at, width):
+        tiles = [ref[at + q] for q in range(width // LANES)]
         return jnp.concatenate(tiles, axis=1)[:6].astype(jnp.bfloat16)
 
-    def learn_row(r, carry):
-        slot = jnp.where((r >= 1) & (r <= 8), r - 1, 8) * 4
-        for c in range(2048 // STEP):
-            cut = pl.ds(c * STEP, STEP)
-            hidden = jnp.tanh(
-                jnp.dot(w1[...], operand(x_ref, r, c), preferred_element_type=jnp.float32)
+    def learn(parts):
+        for at, slot, first, width in parts:
+            h_ref[slot, :, pl.ds(first, width)] = jnp.tanh(
+                jnp.dot(w1, operand(x_ref, at, width), preferred_element_type=jnp.float32)
             ).astype(jnp.bfloat16)
-            h_ref[slot, :, cut] = hidden
-            for k in range(3):
-                hidden = jnp.tanh(
-                    jnp.dot(wm[k], hidden, preferred_element_type=jnp.float32)
+        for k in range(3):
+            for at, slot, first, width in parts:
+                cut = pl.ds(first, width)
+                h_ref[slot + k + 1, :, cut] = jnp.tanh(
+                    jnp.dot(wm[k], h_ref[slot + k, :, cut], preferred_element_type=jnp.float32)
                 ).astype(jnp.bfloat16)
-                h_ref[slot + k + 1, :, cut] = hidden
-            out = jnp.dot(wl[...], hidden, preferred_element_type=jnp.float32)
-            at = r * SEGS + 8 + c * (STEP // LANES)
-            for q in range(STEP // LANES):
+        for at, slot, first, width in parts:
+            out = jnp.dot(wl[...], h_ref[slot + 3, :, pl.ds(first, width)], preferred_element_type=jnp.float32)
+            for q in range(width // LANES):
                 l_ref[at + q, 0:6, :] = out[:, q * LANES : (q + 1) * LANES]
-        return carry
-
-    lax.fori_loop(0, 11, learn_row, 0)
-    for r in range(10):
-        beside = l_ref[10 * SEGS + 8 + r]
-        l_ref[r * SEGS] = beside
-        l_ref[r * SEGS + 7] = beside
-
-    for copy in second_a:
-        copy.wait()
-
-    def choose_row(e, carry):
-        ids = aux[e * 4 + 3].astype(jnp.int32)
-        low, middle, high = (ids & 1) == 1, (ids & 2) == 2, (ids & 4) == 4
-        for k, (a, b) in enumerate(PAIRS):
-            p = [jnp.where(low, stiff[2 * q + 1, a, b], stiff[2 * q, a, b]) for q in range(4)]
-            c_ref[e * 21 + k] = jnp.where(
-                high, jnp.where(middle, p[3], p[2]), jnp.where(middle, p[1], p[0])
-            )
-        return carry
-
-    lax.fori_loop(7, 17, choose_row, 0)
+
+    def row_parts(r, slot):
+        return [
+            (r * SEGS + 8 + c * (STEP // LANES), slot, c * STEP, STEP) for c in range(2048 // STEP)
+        ]
 
     def stress_row(r, carry):
         e = r + 7
@@ -520,37 +519,63 @@
             s_ref[e * 6 + k] = stress[k] + flat(l_ref)[pl.ds(r * (SEGS * 8) + k, SEGS, stride=8), :]
         return carry
 
-    lax.fori_loop(0, 10, stress_row, 0)
-
-    def residual_row(e, carry):
-        force = forces_at(s_ref, e, lane)
-        for f in range(3):
-            v0[e * 3 + f] = (
-                force[f] + aux[e * 4 + f] * dsp[e * 3 + f] - lod[(e - 8) * 3 + f]
-            )
+    learn([(beside, 32, 0, LANES)] + row_parts(0, 36))
+    for r in range(10):
+        turned = pltpu.roll(l_ref[beside], LANES - 1 - 2 * r, 1)
+        l_ref[r * SEGS] = turned
+        l_ref[r * SEGS + 7] = turned
+    learn(row_parts(1, 0))
+    stress_row(0, 0)
+    stress_row(1, 0)
+
+    def rows_of_group(g):
+        own, at = pl.ds(OWN, TILES), g * 6
+        return [
+            send(v0.at[pl.ds(24 + at, 6), own, :], v0.at[pl.ds(at, 6), own, :],
+                 c_s.at[6 + g], c_r.at[6 + g], place(down, 0)),
+            send(v0.at[pl.ds(24 + at, 6), own, :], v0.at[pl.ds(48 + at, 6), own, :],
+                 c_s.at[10 + g], c_r.at[10 + g], place(up, 0)),
+        ]
+
+    def group(g, carry):
+        r = 2 * g + 2
+        learn(row_parts(r, (r - 1) * 4) + row_parts(r + 1, jnp.where(g == 3, 32, r * 4)))
+        for k in range(2):
+            stress_row(r + k, 0)
+        for k in range(2):
+            e = 8 + 2 * g + k
+            force = forces_at(s_ref, e, lane)
+            for f in range(3):
+                v0[e * 3 + f] = force[f] + aux[e * 3 + f] * dsp[e * 3 + f] - lod[(e - 8) * 3 + f]
+        start(rows_of_group(g))
         return carry
 
-    lax.fori_loop(8, 16, residual_row, 0)
+    lax.fori_loop(0, 4, group, 0)
     for side, t in ((0, 0), (1, TILES - 1)):
         for f in range(3):
             edge_c[side, f] = column(v0, 3, f, OWN, 8 + t)[...]
-    moves_c = rows_to(v0, 3, 7, c_s, c_r, 0) + edges_to(edge_c, got_c, c_s, c_r, 2)
+    moves_c = edges_to(edge_c, got_c, c_s, c_r, 0)
     start(moves_c)
-    for t in range(TILES):
-        for f in range(3):
-            res_o[f, :, pl.ds(t * LANES, LANES)] = column(v0, 3, f, OWN, 8 + t)[...]
+    for copy in second_a:
+        copy.wait()
     lax.fori_loop(2, 7, choose_row, 0)
     lax.fori_loop(17, 22, choose_row, 0)
+    for t in range(TILES):
+        for f in range(3):
+            res_o[f, :, pl.ds(t * LANES, LANES)] = column(v0, 3, f, OWN, 8 + t)[...]
     for copy in moves_c:
         copy.wait()
+    for g in range(4):
+        for copy in rows_of_group(g):
+            copy.wait()
     for k, (segment, row) in enumerate(landing):
         for f in range(3):
             column(v0, 3, f, row, segment)[...] = got_c[k, f]
 
     def mean(k):
-        total = stiff[0, k, k]
+        total = stiff[k, 0, k]
         for q in range(1, 8):
-            total = total + stiff[q, k, k]
+            total = total + stiff[k, q, k]
         return total * 0.125
 
     half = 1.0 + 8.0 * jnp.maximum(mean(3), mean(4))
@@ -572,7 +597,7 @@
             force = forces_at(s_ref, e, lane)
             for f in range(3):
                 here = v[e * 3 + f]
-                image = force[f] + aux[e * 4 + f] * here
+                image = force[f] + aux[e * 3 + f] * here
                 if older is None:
                     out[e * 3 + f] = inverse * image - here
                 else:
@@ -598,7 +623,7 @@
         totals = list(totals)
         for f in range(3):
             a, b, c, d = v0[e * 3 + f], v1[e * 3 + f], v2[e * 3 + f], v3[e * 3 + f]
-            energy = energy + aux[e * 4 + f] * (d * d)
+            energy = energy + aux[e * 3 + f] * (d * d)
             for k, product in enumerate((a * a, a * b, b * b, b * c, c * c, c * d, d * d)):
                 totals[k] = totals[k] + folded(product)
         totals[7] = totals[7] + folded(energy)
@@ -610,17 +635,19 @@
     def shared(source, slots, sent, received, count, mine, spot, piece=None):
         copies = []
         for k in range(1, count):
-            to = spot(k)
-            other = lax.rem(mine + k, count)
-            src = source if piece is None else source.at[other]
-            copies.append(send(src, slots.at[mine], sent.at[k], received.at[mine], to))
+            src = source if piece is None else source.at[lax.rem(mine + k, count)]
+            copies.append(send(src, slots.at[mine], sent.at[k], received.at[mine], spot(k)))
         start(copies)
         own = source if piece is None else source.at[mine]
         slots[mine] = own[...]
-        for k in range(1, count):
-            other = lax.rem(mine + k, count)
-            src = source if piece is None else source.at[other]
-            send(src, slots.at[other], sent.at[k], received.at[other], spot(k)).wait()
+
+        def finish():
+            for k in range(1, count):
+                other = lax.rem(mine + k, count)
+                src = source if piece is None else source.at[other]
+                send(src, slots.at[other], sent.at[k], received.at[other], spot(k)).wait()
+
+        return finish
 
     def summed(slots, count):
         total = slots[0]
@@ -629,9 +656,9 @@
         return total
 
     by_sub, by_patch = (lambda k: place(0, k)), (lambda k: place(k, 0))
-    shared(d_out, d_in, d1_s, d1_r, count_s, me_s, by_sub)
+    shared(d_out, d_in, d1_s, d1_r, count_s, me_s, by_sub)()
     d_mid[...] = summed(d_in, count_s)
-    shared(d_mid, d_in2, d2_s, d2_r, count_p, me_p, by_patch)
+    shared(d_mid, d_in2, d2_s, d2_r, count_p, me_p, by_patch)()
     everyone = jnp.sum(summed(d_in2, count_p), axis=1, keepdims=True)
     n = [jnp.broadcast_to(everyone[k : k + 1], (1, LANES)) for k in range(8)]
     n34 = (2.0 * inverse) * n[7] - 2.0 * n[6] - n[5]
@@ -680,7 +707,7 @@
             beta = fresh / norm
             way = [rest[k] + (beta * way[k] if k < len(way) else zero) for k in range(len(rest))]
             norm = fresh
-    trust_o[...] = jnp.broadcast_to(worst, (8, LANES))
+    trust_o[0, 0] = worst[0, 0]
 
     def adjoint_row(e, carry):
         for f in range(3):
@@ -704,40 +731,69 @@
 
     acc_m[...] = jnp.zeros_like(acc_m)
     acc_s[...] = jnp.zeros_like(acc_s)
-    wlt = wl[...].T
-
-    def back_row(r, carry):
-        slot = r * 4
+
+    def derive(weights, signal_of, slot):
         for c in range(2048 // STEP):
             cut = pl.ds(c * STEP, STEP)
-            u = operand(u_ref, r, c)
-            h = h_ref[slot + 3, :, cut]
-            acc_s[0:6] += outer_product(u, h)
-            signal = jnp.dot(wlt, u, preferred_element_type=jnp.float32)
-            d = (signal * (1.0 - jnp.square(h.astype(jnp.float32)))).astype(jnp.bfloat16)
-            for k in range(2, -1, -1):
-                h = h_ref[slot + k, :, cut]
-                acc_m[pl.ds(k * 128, 128)] += outer_product(d, h)
-                signal = jnp.dot(wmt[k], d, preferred_element_type=jnp.float32)
-                d = (signal * (1.0 - jnp.square(h.astype(jnp.float32)))).astype(jnp.bfloat16)
-            acc_s[8:14] += outer_product(operand(x_ref, r + 1, c), d)
+            h = h_ref[slot, :, cut].astype(jnp.float32)
+            signal = jnp.dot(weights, signal_of(c, cut), preferred_element_type=jnp.float32)
+            h_ref[slot, :, cut] = (signal * (1.0 - jnp.square(h))).astype(jnp.bfloat16)
+
+    def back_last(r, carry):
+        slot = r * 4 + 3
+        u = operand(u_ref, r * SEGS + 8, 2048)
+        acc_s[0:6] += outer_product(u, h_ref[slot])
+        derive(wlt, lambda c, cut: u[:, c * STEP : (c + 1) * STEP], slot)
         return carry
 
-    lax.fori_loop(0, 8, back_row, 0)
-
-    whole = jnp.concatenate([acc_m[...], acc_s[...]], axis=0)
+    def back_mid(k):
+        def body(r, carry):
+            slot = r * 4 + k
+            acc_m[k] += outer_product(h_ref[slot + 1], h_ref[slot])
+            derive(wmt[k], lambda c, cut: h_ref[slot + 1, :, cut], slot)
+            return carry
+
+        lax.fori_loop(0, 8, body, 0)
+
+    def back_first(r, carry):
+        acc_s[8:14] += outer_product(operand(x_ref, (r + 1) * SEGS + 8, 2048), h_ref[r * 4])
+        return carry
+
+    lax.fori_loop(0, 8, back_last, 0)
+    back_mid(2)
+    back_mid(1)
     for k in range(16):
-        e_out[k, 0:25, :] = whole[25 * k : 25 * (k + 1)]
-    shared(e_out, e_in, e1_s, e1_r, count_s, me_s, by_sub, piece=True)
+        e_out[k, 0:8, :] = acc_m[1, 8 * k : 8 * k + 8]
+        e_out[k, 8:16, :] = acc_m[2, 8 * k : 8 * k + 8]
+    finish_e1 = shared(e_out, e_in, e1_s, e1_r, count_s, me_s, by_sub, piece=True)
+    back_mid(0)
+    finish_e1()
     e_mid[...] = summed(e_in, count_s)
-    shared(e_mid, e_in2, e2_s, e2_r, count_p, me_p, by_patch)
+    finish_e2 = shared(e_mid, e_in2, e2_s, e2_r, count_p, me_p, by_patch)
+    lax.fori_loop(0, 8, back_first, 0)
+    for k in range(16):
+        g_out[k, 0:8, :] = acc_m[0, 8 * k : 8 * k + 8]
+        g_out[k, 8:9, :] = acc_s[k : k + 1]
+    finish_g1 = shared(g_out, g_in, g1_s, g1_r, count_s, me_s, by_sub, piece=True)
+    finish_g1()
+    g_mid[...] = summed(g_in, count_s)
+    finish_g2 = shared(g_mid, g_in2, g2_s, g2_r, count_p, me_p, by_patch)
+    finish_e2()
     e_end[...] = summed(e_in2, count_p)
-    shared(e_end, e_in3, e3_s, e3_r, count_s, me_s, by_sub)
-    whole = jnp.concatenate([e_in3[k, 0:25, :] for k in range(16)], axis=0)
-    for k in range(3):
-        gm_o[k] = whole[128 * k : 128 * (k + 1)]
-    gl_o[...] = whole[384:390]
-    gf_o[...] = whole[392:400].T[:, 0:6]
+    finish_e3 = shared(e_end, e_in3, e3_s, e3_r, count_s, me_s, by_sub)
+    finish_g2()
+    g_end[...] = summed(g_in2, count_p)
+    finish_g3 = shared(g_end, g_in3, g3_s, g3_r, count_s, me_s, by_sub)
+    finish_e3()
+    for k in range(16):
+        gm_o[1, 8 * k : 8 * k + 8] = e_in3[k, 0:8, :]
+        gm_o[2, 8 * k : 8 * k + 8] = e_in3[k, 8:16, :]
+    finish_g3()
+    for k in range(16):
+        gm_o[0, 8 * k : 8 * k + 8] = g_in3[k, 0:8, :]
+    for k in range(6):
+        gl_o[k : k + 1] = g_in3[k, 8:9, :]
+        gf_o[k : k + 1] = g_in3[8 + k, 8:9, :]
 
 
 def per_device(displacement, load, foundation, layup, layup_stiffness, w_first, w_mid, w_last):
@@ -754,38 +810,42 @@
         out_shape=[
             jax.ShapeDtypeStruct(displacement.shape, f32),
             jax.ShapeDtypeStruct(displacement.shape, f32),
-            jax.ShapeDtypeStruct((128, 6), f32),
+            jax.ShapeDtypeStruct((6, 128), f32),
             jax.ShapeDtypeStruct((3, 128, 128), f32),
             jax.ShapeDtypeStruct((6, 128), f32),
-            jax.ShapeDtypeStruct((8, LANES), f32),
+            jax.ShapeDtypeStruct((1, 1), f32),
         ],
         in_specs=[vmem] * 4 + [smem] + [vmem] * 3,
-        out_specs=[vmem] * 6,
+        out_specs=[vmem] * 5 + [smem],
         scratch_shapes=[
-            rows(3), rows(4), rows(3, 8),
+            rows(3), rows(3), rows(1), rows(3, 8),
             pltpu.VMEM((2, 7, 8, LANES), f32), pltpu.VMEM((2, 3, 8, LANES), f32),
             pltpu.VMEM((6, 7, 8, LANES), f32), pltpu.VMEM((6, 3, 8, LANES), f32),
             rows(7), rows(6), rows(21),
             pltpu.VMEM((11 * SEGS, 8, LANES), f32),
             pltpu.VMEM((11 * SEGS, 8, LANES), f32),
             pltpu.VMEM((8 * SEGS, 8, LANES), f32),
-            pltpu.VMEM((9 * 4, 128, 2048), bf16),
+            pltpu.VMEM((10 * 4, 128, 2048), bf16),
             rows(3), rows(3), rows(3), rows(3),
             pltpu.VMEM((3, 128, 128), bf16),
-            pltpu.VMEM((384, 128), f32), pltpu.VMEM((16, 128), f32),
+            pltpu.VMEM((3, 128, 128), f32), pltpu.VMEM((16, 128), f32),
             pltpu.VMEM((8, LANES), f32), pltpu.VMEM((16, 8, LANES), f32),
             pltpu.VMEM((8, LANES), f32), pltpu.VMEM((16, 8, LANES), f32),
-            pltpu.VMEM((16, 32, LANES), f32), pltpu.VMEM((16, 32, LANES), f32),
-            pltpu.VMEM((32, LANES), f32), pltpu.VMEM((16, 32, LANES), f32),
-            pltpu.VMEM((32, LANES), f32), pltpu.VMEM((16, 32, LANES), f32),
-            dma((10,)), dma((10,)), dma((8,)), dma((8,)),
-        ] + [dma((16,)) for _ in range(10)],
+        ] + [
+            pltpu.VMEM(shape, f32)
+            for n in (16, 9)
+            for shape in [(16, n, LANES), (16, n, LANES), (n, LANES)] + [(16, n, LANES), (n, LANES), (16, n, LANES)]
+        ] + [
+            dma((14,)), dma((14,)), dma((14,)), dma((14,)),
+        ] + [dma((16,)) for _ in range(16)],
         compiler_params=pltpu.CompilerParams(
-            collective_id=0, has_side_effects=True, vmem_limit_bytes=60 << 20
+            collective_id=0, has_side_effects=True, vmem_limit_bytes=52 << 20
         ),
         name="adjoint_step",
-    )(displacement, load, foundation, layup, layup_stiffness, w_first, w_mid, w_last)
-    fast, trust = tuple(out[:5]), out[5][0, 0]
+    )(
+        displacement, load, foundation, layup, layup_stiffness.transpose(1, 0, 2), w_first.T, w_mid, w_last
+    )
+    fast, trust = (out[0], out[1], out[2].T, out[3], out[4]), out[5][0, 0]
     operands = (displacement, load, foundation, layup, layup_stiffness, w_first, w_mid, w_last)
     return lax.cond(trust <= TRUST, lambda: fast, lambda: careful(*operands))
 

time: 147 us -> 104 us (0.71)
  Pallas kernels: 135 us -> 97.6 us
  local copies, waits for them, and re-layouts: 9.39 us -> 5.09 us
    pallas_call x1, Pallas kernels: 135 us -> 97.6 us  [per_device(): pl.pallas_call(fused, out_shape=[jax.ShapeDtypeStruct(displacement.shape,...]
    unnamed x8 -> x5, local copies, waits for them, and re-layouts: 7.3 us -> 5.09 us
where the time goes in v2:
time: 104 us
  Pallas kernels  97.6 us (94%)
  local copies, waits for them, and re-layouts  5.09 us (5%)
  between operations  1.22 us (1%)
    pallas_call x1, Pallas kernels, per_device(): pl.pallas_call(fused, out_shape=[jax.ShapeDtypeStruct(displacement.shape,...  97.6 us
    unnamed x5, local copies, waits for them, and re-layouts  5.09 us

profile of v2, /device:TPU:1, one launch (start us, length us, event | category | flops | bytes accessed | tf_op | source)
XLA Modules:
  0.0 104.2 jit_solution(3515299358575223515)
XLA Ops:
  0.6 97.6 %adjoint_step.1 = (f32[3,8,2048]{2,1,0:T(8,128)S(1)}, f32[3,8,2048]{2,1,0:T(8,128)}, f32[6,128]{1,0:T(8,128)S(1)}, f32[3,128,128]{2,1,0:T(8,128)}, f32[6,128]{1,0:T(8,128)S(1)}, /*index=5*/f32[1,1]{1,0:T(1,128)}) custom-call(f32[3,8,2048]{2,1,0:T(8,128)} %disp.1, f32[3,8,2048]{2,1,0:T(8,128)} %load.1, f32[3,8,2048]{2,1,0:T(8,128)} %found.1, s32[8,2048]{1,0:T(8,128)} %lay.1, ...), custom_call_target="tpu_custom_call" | custom-call | tf_op jit(solution)/shard_map/adjoint_step/pallas_call | solution.py:808
  98.8 0.2 conditional.1
  99.1 0.7 copy.548
  99.7 1.6 %copy.549 = f32[3,8,2048]{2,1,0:T(8,128)} copy(f32[3,8,2048]{2,1,0:T(8,128)} %get-tuple-element.451) | data formatting | bytes 393216
  101.3 0.6 copy.550
  101.9 1.6 %copy.551 = f32[3,128,128]{2,1,0:T(8,128)} copy(f32[3,128,128]{2,1,0:T(8,128)} %get-tuple-element.453) | data formatting | bytes 393216
  103.6 0.6 copy.552

commit v3 on v2

--- a/solution.py
+++ b/solution.py
@@ -359,9 +359,9 @@
 
 
 def fused(
-    disp, load, found, lay, stiff, w1t, wm, wl,
+    disp_in, load_in, found_in, lay_in, stiff, w1t, wm, wl,
     res_o, adj_o, gf_o, gm_o, gl_o, trust_o,
-    dsp, aux, ids, lod, edge_a, edge_c, got_a, got_c, y_ref, s_ref, c_ref, x_ref, l_ref, u_ref, h_ref,
+    disp, load, found, lay, in_s, dsp, aux, ids, lod, edge_a, edge_c, got_a, got_c, y_ref, s_ref, c_ref, x_ref, l_ref, u_ref, h_ref,
     v0, v1, v2, v3, wmt, acc_m, acc_s,
     d_out, d_in, d_mid, d_in2, e_out, e_in, e_mid, e_in2, e_end, e_in3,
     g_out, g_in, g_mid, g_in2, g_end, g_in3,
@@ -382,6 +382,15 @@
     for dp, ds in greeted:
         pl.semaphore_signal(barrier, inc=1, device_id=place(dp, ds), device_id_type=MESH)
 
+    arriving = [
+        pltpu.make_async_copy(source, held, in_s.at[k])
+        for k, (source, held) in enumerate(((disp_in, disp), (lay_in, lay), (found_in, found), (load_in, load)))
+    ]
+    for copy in arriving:
+        copy.start()
+    for copy in arriving[:3]:
+        copy.wait()
+
     for t in range(TILES):
         cut = pl.ds(t * LANES, LANES)
         for f in range(3):
@@ -391,8 +400,8 @@
     for side, cut in ends:
         for f in range(3):
             edge_a[side, f] = disp[f, :, cut]
-            edge_a[side, 3 + f] = found[f, :, cut]
-        edge_a[side, 6] = lay[:, cut].astype(jnp.float32)
+            edge_a[side, 4 + f] = found[f, :, cut]
+        edge_a[side, 3] = lay[:, cut].astype(jnp.float32)
 
     pl.semaphore_wait(barrier, len(greeted))
 
@@ -417,10 +426,10 @@
 
     heading = ((0, right, 1), (0, left, 0), (down, right, 1), (down, left, 0), (up, right, 1), (up, left, 0))
 
-    def edges_to(edge, got, sent, received, first):
+    def edges_to(edge, got, fields, sent, received, first):
         return [
-            send(edge.at[side], got.at[k], sent.at[first + k], received.at[first + k], place(dp, ds))
-            for k, (dp, ds, side) in enumerate(heading)
+            send(edge.at[side, fields], got.at[k, fields], sent.at[first + k], received.at[first + k], place(dp, ds))
+            for k, (dp, ds, side) in reversed(list(enumerate(heading)))
         ]
 
     def start(copies):
@@ -430,11 +439,12 @@
     landing = ((7, 8), (0, 8), (7, 0), (0, 0), (7, 16), (0, 16))
 
     first_a = (
-        rows_to(dsp, 3, 0, 2, a_s, a_r, 0)
-        + edges_to(edge_a, got_a, a_s, a_r, 2)
+        edges_to(edge_a, got_a, pl.ds(0, 4), a_s, a_r, 2)
+        + rows_to(dsp, 3, 0, 2, a_s, a_r, 0)
         + rows_to(ids, 1, 0, 1, a_s, a_r, 8)
     )
     start(first_a)
+    arriving[3].wait()
     for t in range(TILES):
         cut = pl.ds(t * LANES, LANES)
         for f in range(3):
@@ -457,14 +467,16 @@
 
     for copy in first_a:
         copy.wait()
+    second_a = (
+        rows_to(aux, 3, 0, 5, a_s, a_r, 10)
+        + rows_to(ids, 1, 1, 6, a_s, a_r, 12)
+        + edges_to(edge_a, got_a, pl.ds(4, 3), a_s, a_r, 14)
+    )
+    start(second_a)
     for k, (segment, row) in enumerate(landing):
         for f in range(3):
             column(dsp, 3, f, row, segment)[...] = got_a[k, f]
-            column(aux, 3, f, row, segment)[...] = got_a[k, 3 + f]
-        column(ids, 1, 0, row, segment)[...] = got_a[k, 6]
-    second_a = rows_to(aux, 3, 0, 5, a_s, a_r, 10) + rows_to(ids, 1, 1, 6, a_s, a_r, 12)
-    start(second_a)
-    lax.fori_loop(7, 17, choose_row, 0)
+        column(ids, 1, 0, row, segment)[...] = got_a[k, 3]
 
     lane = lane_of()
     along_columns(lambda e: [dsp[e * 3 + f] for f in range(3)], y_ref, 6, 18)
@@ -512,52 +524,59 @@
             (r * SEGS + 8 + c * (STEP // LANES), slot, c * STEP, STEP) for c in range(2048 // STEP)
         ]
 
-    def stress_row(r, carry):
+    def stress_row(r):
         e = r + 7
+        choose_row(e, 0)
         stress = laminate(c_ref, e, [s_ref[e * 6 + k] for k in range(6)])
         for k in range(6):
             s_ref[e * 6 + k] = stress[k] + flat(l_ref)[pl.ds(r * (SEGS * 8) + k, SEGS, stride=8), :]
-        return carry
+
+    def residual_row(e):
+        force = forces_at(s_ref, e, lane)
+        for f in range(3):
+            v0[e * 3 + f] = force[f] + aux[e * 3 + f] * dsp[e * 3 + f] - lod[(e - 8) * 3 + f]
+
+    def residual_to(e):
+        own, row = pl.ds(OWN, TILES), v0.at[pl.ds(e * 3, 3), pl.ds(OWN, TILES), :]
+        return [
+            send(row, v0.at[pl.ds((e - 8) * 3, 3), own, :], c_s.at[e - 2], c_r.at[e - 2], place(down, 0)),
+            send(row, v0.at[pl.ds((e + 8) * 3, 3), own, :], c_s.at[e + 6], c_r.at[e + 6], place(up, 0)),
+        ]
 
     learn([(beside, 32, 0, LANES)] + row_parts(0, 36))
     for r in range(10):
         turned = pltpu.roll(l_ref[beside], LANES - 1 - 2 * r, 1)
         l_ref[r * SEGS] = turned
         l_ref[r * SEGS + 7] = turned
-    learn(row_parts(1, 0))
-    stress_row(0, 0)
-    stress_row(1, 0)
-
-    def rows_of_group(g):
-        own, at = pl.ds(OWN, TILES), g * 6
-        return [
-            send(v0.at[pl.ds(24 + at, 6), own, :], v0.at[pl.ds(at, 6), own, :],
-                 c_s.at[6 + g], c_r.at[6 + g], place(down, 0)),
-            send(v0.at[pl.ds(24 + at, 6), own, :], v0.at[pl.ds(48 + at, 6), own, :],
-                 c_s.at[10 + g], c_r.at[10 + g], place(up, 0)),
-        ]
-
-    def group(g, carry):
-        r = 2 * g + 2
-        learn(row_parts(r, (r - 1) * 4) + row_parts(r + 1, jnp.where(g == 3, 32, r * 4)))
-        for k in range(2):
-            stress_row(r + k, 0)
-        for k in range(2):
-            e = 8 + 2 * g + k
-            force = forces_at(s_ref, e, lane)
-            for f in range(3):
-                v0[e * 3 + f] = force[f] + aux[e * 3 + f] * dsp[e * 3 + f] - lod[(e - 8) * 3 + f]
-        start(rows_of_group(g))
+    for r in (1, 2):
+        stress_row(r - 1)
+        learn(row_parts(r, (r - 1) * 4))
+
+    def pipelined_row(r, carry):
+        @pl.when(r > 3)
+        def _():
+            start(residual_to(r + 4))
+
+        stress_row(r - 1)
+        residual_row(r + 5)
+        learn(row_parts(r, (r - 1) * 4))
         return carry
 
-    lax.fori_loop(0, 4, group, 0)
+    lax.fori_loop(3, 10, pipelined_row, 0)
+    start(residual_to(14))
+    stress_row(9)
+    residual_row(15)
+    start(residual_to(15))
     for side, t in ((0, 0), (1, TILES - 1)):
         for f in range(3):
             edge_c[side, f] = column(v0, 3, f, OWN, 8 + t)[...]
-    moves_c = edges_to(edge_c, got_c, c_s, c_r, 0)
+    moves_c = edges_to(edge_c, got_c, pl.ds(0, 3), c_s, c_r, 0)
     start(moves_c)
     for copy in second_a:
         copy.wait()
+    for k, (segment, row) in enumerate(landing):
+        for f in range(3):
+            column(aux, 3, f, row, segment)[...] = got_a[k, 4 + f]
     lax.fori_loop(2, 7, choose_row, 0)
     lax.fori_loop(17, 22, choose_row, 0)
     for t in range(TILES):
@@ -565,8 +584,8 @@
             res_o[f, :, pl.ds(t * LANES, LANES)] = column(v0, 3, f, OWN, 8 + t)[...]
     for copy in moves_c:
         copy.wait()
-    for g in range(4):
-        for copy in rows_of_group(g):
+    for e in range(8, 16):
+        for copy in residual_to(e):
             copy.wait()
     for k, (segment, row) in enumerate(landing):
         for f in range(3):
@@ -591,7 +610,7 @@
                 s_ref[e * 6 + k] = stress[k]
             return carry
 
-        lax.fori_loop(first - 1, last + 1, body, 0)
+        lax.fori_loop(first - 1, last + 1, body, 0, unroll=2)
 
         def finish(e, carry):
             force = forces_at(s_ref, e, lane)
@@ -604,7 +623,7 @@
                     out[e * 3 + f] = (2.0 * inverse) * image - 2.0 * here - older[e * 3 + f]
             return carry
 
-        lax.fori_loop(first, last, finish, 0)
+        lax.fori_loop(first, last, finish, 0, unroll=2)
 
     apply_stiffness(v0, None, v1, 3, 21)
     apply_stiffness(v1, v0, v2, 5, 19)
@@ -767,14 +786,14 @@
         e_out[k, 8:16, :] = acc_m[2, 8 * k : 8 * k + 8]
     finish_e1 = shared(e_out, e_in, e1_s, e1_r, count_s, me_s, by_sub, piece=True)
     back_mid(0)
-    finish_e1()
-    e_mid[...] = summed(e_in, count_s)
-    finish_e2 = shared(e_mid, e_in2, e2_s, e2_r, count_p, me_p, by_patch)
     lax.fori_loop(0, 8, back_first, 0)
     for k in range(16):
         g_out[k, 0:8, :] = acc_m[0, 8 * k : 8 * k + 8]
         g_out[k, 8:9, :] = acc_s[k : k + 1]
     finish_g1 = shared(g_out, g_in, g1_s, g1_r, count_s, me_s, by_sub, piece=True)
+    finish_e1()
+    e_mid[...] = summed(e_in, count_s)
+    finish_e2 = shared(e_mid, e_in2, e2_s, e2_r, count_p, me_p, by_patch)
     finish_g1()
     g_mid[...] = summed(g_in, count_s)
     finish_g2 = shared(g_mid, g_in2, g2_s, g2_r, count_p, me_p, by_patch)
@@ -815,9 +834,11 @@
             jax.ShapeDtypeStruct((6, 128), f32),
             jax.ShapeDtypeStruct((1, 1), f32),
         ],
-        in_specs=[vmem] * 4 + [smem] + [vmem] * 3,
+        in_specs=[pl.BlockSpec(memory_space=pl.ANY)] * 4 + [smem] + [vmem] * 3,
         out_specs=[vmem] * 5 + [smem],
         scratch_shapes=[
+            pltpu.VMEM(displacement.shape, f32), pltpu.VMEM(displacement.shape, f32),
+            pltpu.VMEM(displacement.shape, f32), pltpu.VMEM(layup.shape, jnp.int32), dma((4,)),
             rows(3), rows(3), rows(1), rows(3, 8),
             pltpu.VMEM((2, 7, 8, LANES), f32), pltpu.VMEM((2, 3, 8, LANES), f32),
             pltpu.VMEM((6, 7, 8, LANES), f32), pltpu.VMEM((6, 3, 8, LANES), f32),
@@ -836,10 +857,10 @@
             for n in (16, 9)
             for shape in [(16, n, LANES), (16, n, LANES), (n, LANES)] + [(16, n, LANES), (n, LANES), (16, n, LANES)]
         ] + [
-            dma((14,)), dma((14,)), dma((14,)), dma((14,)),
+            dma((20,)), dma((20,)), dma((22,)), dma((22,)),
         ] + [dma((16,)) for _ in range(16)],
         compiler_params=pltpu.CompilerParams(
-            collective_id=0, has_side_effects=True, vmem_limit_bytes=52 << 20
+            collective_id=0, has_side_effects=True, vmem_limit_bytes=46 << 20
         ),
         name="adjoint_step",
     )(

time: 104 us -> 102 us (0.981)
  Pallas kernels: 97.6 us -> 95 us
    pallas_call x1, Pallas kernels: 97.6 us -> 95 us  [per_device(): pl.pallas_call(fused, out_shape=[jax.ShapeDtypeStruct(displacement.shape,...]
where the time goes in v3:
time: 102 us
  Pallas kernels  95 us (93%)
  local copies, waits for them, and re-layouts  5.09 us (5%)
  between operations  1.22 us (1%)
    pallas_call x1, Pallas kernels, per_device(): pl.pallas_call(fused, out_shape=[jax.ShapeDtypeStruct(displacement.shape,...  95 us
    unnamed x5, local copies, waits for them, and re-layouts  5.09 us

profile of v3, /device:TPU:1, one launch (start us, length us, event | category | flops | bytes accessed | tf_op | source)
XLA Modules:
  0.0 101.5 jit_solution(5476044575965547989)
XLA Ops:
  0.6 95.0 %adjoint_step.1 = (f32[3,8,2048]{2,1,0:T(8,128)S(1)}, f32[3,8,2048]{2,1,0:T(8,128)}, f32[6,128]{1,0:T(8,128)S(1)}, f32[3,128,128]{2,1,0:T(8,128)}, f32[6,128]{1,0:T(8,128)S(1)}, /*index=5*/f32[1,1]{1,0:T(1,128)}) custom-call(f32[3,8,2048]{2,1,0:T(8,128)} %disp_in.1, f32[3,8,2048]{2,1,0:T(8,128)} %load_in.1, f32[3,8,2048]{2,1,0:T(8,128)} %found_in.1, ...), custom_call_target="tpu_custom_call" | custom-call | tf_op jit(solution)/shard_map/adjoint_step/pallas_call | solution.py:827
  96.2 0.2 conditional.1
  96.4 0.7 copy.548
  97.1 1.6 %copy.549 = f32[3,8,2048]{2,1,0:T(8,128)} copy(f32[3,8,2048]{2,1,0:T(8,128)} %get-tuple-element.451) | data formatting | bytes 393216
  98.7 0.6 copy.550
  99.3 1.6 %copy.551 = f32[3,128,128]{2,1,0:T(8,128)} copy(f32[3,128,128]{2,1,0:T(8,128)} %get-tuple-element.453) | data formatting | bytes 393216
  100.9 0.6 copy.552

commit v4 on v3

--- a/solution.py
+++ b/solution.py
@@ -489,7 +489,7 @@
             flat(x_ref)[pl.ds(r * (SEGS * 8) + k, SEGS, stride=8), :] = strain[k]
         return carry
 
-    lax.fori_loop(0, 10, strain_row, 0)
+    lax.fori_loop(0, 10, strain_row, 0, unroll=2)
     tile_lane = lax.broadcasted_iota(jnp.int32, (8, LANES), 1)
     beside = 10 * SEGS
     packed = jnp.zeros((8, LANES), jnp.float32)
@@ -648,12 +648,15 @@
         totals[7] = totals[7] + folded(energy)
         return tuple(totals)
 
-    totals = lax.fori_loop(8, 16, sums_row, tuple(jnp.zeros((8, LANES), jnp.float32) for _ in range(8)))
+    totals = lax.fori_loop(8, 16, sums_row, tuple(jnp.zeros((8, LANES), jnp.float32) for _ in range(8)), unroll=2)
     d_out[...] = jnp.concatenate([jnp.sum(t, axis=0, keepdims=True) for t in totals], axis=0)
+
+    def farthest_first(count):
+        return sorted(range(1, count), key=lambda k: (-min(k, count - k) - 2 * (k % 2), k))
 
     def shared(source, slots, sent, received, count, mine, spot, piece=None):
         copies = []
-        for k in range(1, count):
+        for k in farthest_first(count):
             src = source if piece is None else source.at[lax.rem(mine + k, count)]
             copies.append(send(src, slots.at[mine], sent.at[k], received.at[mine], spot(k)))
         start(copies)
@@ -734,7 +737,7 @@
             v0[at] = found_y[0] * v0[at] + found_y[1] * v1[at] + found_y[2] * v2[at] + found_y[3] * v3[at]
         return carry
 
-    lax.fori_loop(7, 17, adjoint_row, 0)
+    lax.fori_loop(7, 17, adjoint_row, 0, unroll=2)
     for t in range(TILES):
         for f in range(3):
             adj_o[f, :, pl.ds(t * LANES, LANES)] = column(v0, 3, f, OWN, 8 + t)[...]
@@ -746,7 +749,7 @@
             flat(u_ref)[pl.ds((e - 8) * (SEGS * 8) + k, SEGS, stride=8), :] = strain[k]
         return carry
 
-    lax.fori_loop(8, 16, upstream_row, 0)
+    lax.fori_loop(8, 16, upstream_row, 0, unroll=2)
 
     acc_m[...] = jnp.zeros_like(acc_m)
     acc_s[...] = jnp.zeros_like(acc_s)
@@ -786,7 +789,7 @@
         e_out[k, 8:16, :] = acc_m[2, 8 * k : 8 * k + 8]
     finish_e1 = shared(e_out, e_in, e1_s, e1_r, count_s, me_s, by_sub, piece=True)
     back_mid(0)
-    lax.fori_loop(0, 8, back_first, 0)
+    lax.fori_loop(0, 8, back_first, 0, unroll=2)
     for k in range(16):
         g_out[k, 0:8, :] = acc_m[0, 8 * k : 8 * k + 8]
         g_out[k, 8:9, :] = acc_s[k : k + 1]

time: 102 us -> 100 us (0.980)
  Pallas kernels: 95 us -> 93.6 us
    pallas_call x1, Pallas kernels: 95 us -> 93.6 us  [per_device(): pl.pallas_call(fused, out_shape=[jax.ShapeDtypeStruct(displacement.shape,...]
where the time goes in v4:
time: 100 us
  Pallas kernels  93.6 us (94%)
  local copies, waits for them, and re-layouts  5.09 us (5%)
  between operations  1.22 us (1%)
    pallas_call x1, Pallas kernels, per_device(): pl.pallas_call(fused, out_shape=[jax.ShapeDtypeStruct(displacement.shape,...  93.6 us
    unnamed x5, local copies, waits for them, and re-layouts  5.09 us

profile of v4, /device:TPU:1, one launch (start us, length us, event | category | flops | bytes accessed | tf_op | source)
XLA Modules:
  0.0 100.1 jit_solution(2397457368767008102)
XLA Ops:
  0.6 93.6 %adjoint_step.1 = (f32[3,8,2048]{2,1,0:T(8,128)S(1)}, f32[3,8,2048]{2,1,0:T(8,128)}, f32[6,128]{1,0:T(8,128)S(1)}, f32[3,128,128]{2,1,0:T(8,128)}, f32[6,128]{1,0:T(8,128)S(1)}, /*index=5*/f32[1,1]{1,0:T(1,128)}) custom-call(f32[3,8,2048]{2,1,0:T(8,128)} %disp_in.1, f32[3,8,2048]{2,1,0:T(8,128)} %load_in.1, f32[3,8,2048]{2,1,0:T(8,128)} %found_in.1, ...), custom_call_target="tpu_custom_call" | custom-call | tf_op jit(solution)/shard_map/adjoint_step/pallas_call | solution.py:830
  94.8 0.2 conditional.1
  95.0 0.7 copy.548
  95.7 1.6 %copy.549 = f32[3,8,2048]{2,1,0:T(8,128)} copy(f32[3,8,2048]{2,1,0:T(8,128)} %get-tuple-element.451) | data formatting | bytes 393216
  97.3 0.6 copy.550
  97.9 1.6 %copy.551 = f32[3,128,128]{2,1,0:T(8,128)} copy(f32[3,128,128]{2,1,0:T(8,128)} %get-tuple-element.453) | data formatting | bytes 393216
  99.5 0.6 copy.552

commit v5 on v4

--- a/solution.py
+++ b/solution.py
@@ -649,7 +649,12 @@
         return tuple(totals)
 
     totals = lax.fori_loop(8, 16, sums_row, tuple(jnp.zeros((8, LANES), jnp.float32) for _ in range(8)), unroll=2)
-    d_out[...] = jnp.concatenate([jnp.sum(t, axis=0, keepdims=True) for t in totals], axis=0)
+    spots = lax.broadcasted_iota(jnp.int32, (1, LANES), 1)
+    row = jnp.zeros((1, LANES), jnp.float32)
+    for k, t in enumerate(totals):
+        whole = jnp.sum(jnp.sum(t, axis=0, keepdims=True), axis=1, keepdims=True)
+        row = jnp.where(spots == k, whole, row)
+    d_out[...] = row
 
     def farthest_first(count):
         return sorted(range(1, count), key=lambda k: (-min(k, count - k) - 2 * (k % 2), k))
@@ -681,8 +686,8 @@
     shared(d_out, d_in, d1_s, d1_r, count_s, me_s, by_sub)()
     d_mid[...] = summed(d_in, count_s)
     shared(d_mid, d_in2, d2_s, d2_r, count_p, me_p, by_patch)()
-    everyone = jnp.sum(summed(d_in2, count_p), axis=1, keepdims=True)
-    n = [jnp.broadcast_to(everyone[k : k + 1], (1, LANES)) for k in range(8)]
+    everyone = summed(d_in2, count_p)
+    n = [jnp.broadcast_to(everyone[:, k : k + 1], (1, LANES)) for k in range(8)]
     n34 = (2.0 * inverse) * n[7] - 2.0 * n[6] - n[5]
     m = [n[0], n[1]]
     for k in (2, 3, 4, 5, 6):
@@ -853,8 +858,8 @@
             rows(3), rows(3), rows(3), rows(3),
             pltpu.VMEM((3, 128, 128), bf16),
             pltpu.VMEM((3, 128, 128), f32), pltpu.VMEM((16, 128), f32),
-            pltpu.VMEM((8, LANES), f32), pltpu.VMEM((16, 8, LANES), f32),
-            pltpu.VMEM((8, LANES), f32), pltpu.VMEM((16, 8, LANES), f32),
+            pltpu.VMEM((1, LANES), f32), pltpu.VMEM((16, 1, LANES), f32),
+            pltpu.VMEM((1, LANES), f32), pltpu.VMEM((16, 1, LANES), f32),
         ] + [
             pltpu.VMEM(shape, f32)
             for n in (16, 9)

time: 100 us -> 99.6 us (level)
  no operation moved by 1% of the time
where the time goes in v5:
time: 99.6 us; the launch traced here: 99.4 us
  Pallas kernels  92.9 us (93%)
  local copies, waits for them, and re-layouts  5.09 us (5%)
  between operations  1.22 us (1%)
    pallas_call x1, Pallas kernels, per_device(): pl.pallas_call(fused, out_shape=[jax.ShapeDtypeStruct(displacement.shape,...  92.9 us
    unnamed x5, local copies, waits for them, and re-layouts  5.09 us

profile of v5, /device:TPU:1, one launch (start us, length us, event | category | flops | bytes accessed | tf_op | source)
XLA Modules:
  0.0 99.4 jit_solution(2102653903744303935)
XLA Ops:
  0.6 92.9 %adjoint_step.1 = (f32[3,8,2048]{2,1,0:T(8,128)S(1)}, f32[3,8,2048]{2,1,0:T(8,128)}, f32[6,128]{1,0:T(8,128)S(1)}, f32[3,128,128]{2,1,0:T(8,128)}, f32[6,128]{1,0:T(8,128)S(1)}, /*index=5*/f32[1,1]{1,0:T(1,128)}) custom-call(f32[3,8,2048]{2,1,0:T(8,128)} %disp_in.1, f32[3,8,2048]{2,1,0:T(8,128)} %load_in.1, f32[3,8,2048]{2,1,0:T(8,128)} %found_in.1, ...), custom_call_target="tpu_custom_call" | custom-call | tf_op jit(solution)/shard_map/adjoint_step/pallas_call | solution.py:835
  94.1 0.2 conditional.1
  94.3 0.7 copy.548
  95.0 1.6 %copy.549 = f32[3,8,2048]{2,1,0:T(8,128)} copy(f32[3,8,2048]{2,1,0:T(8,128)} %get-tuple-element.451) | data formatting | bytes 393216
  96.6 0.6 copy.550
  97.2 1.6 %copy.551 = f32[3,128,128]{2,1,0:T(8,128)} copy(f32[3,128,128]{2,1,0:T(8,128)} %get-tuple-element.453) | data formatting | bytes 393216
  98.8 0.6 copy.552
